TPU v7x, 512 devices: a whole 4x8x8 slice. The times are simulated.
512 devices in a mesh: grp: 16 (over x_lo, z), fsdp: 32 (over y, x_hi, core).
Axes of the slice: x: 4 (x_hi: 2, x_lo: 2; x = x_hi * 2 + x_lo), y: 8, z: 8, core: 2. Of those that a mesh axis runs over, the one named last changes fastest.
Arguments:
- weight: float32 [16, 4608, 256], P('grp', 'fsdp'), may hold values from -6 to 6
- momentum: float32 [16, 4608, 256], P('grp', 'fsdp'), may hold values from -4 to 4
- adam_mean: float32 [16, 4608, 256], P('grp', 'fsdp'), may hold values from -0.00048828125 to 0.00048828125
- adam_var: float32 [16, 4608, 256], P('grp', 'fsdp'), may hold values from 1.0007694e-09 to 1.0007693e-08
- inputs: bfloat16 [16, 8192, 4608], P('grp', 'fsdp'), may hold values from -6 to 6
- targets: bfloat16 [16, 8192, 256], P('grp', 'fsdp'), may hold values from -6 to 6
- states: bfloat16 [16, 4096, 4608], P('grp', 'fsdp'), may hold values from -6 to 6
- partner: int32 [16, 32], P(None, 'fsdp'), may hold values from 0 to 15, as said below
Outputs:
- new_weight: float32 [16, 4608, 256], P('grp', 'fsdp')
- new_momentum: float32 [16, 4608, 256], P('grp', 'fsdp')
- rollout_keys: bfloat16 [16, 4096, 256], P('grp', 'fsdp')
Inputs may be any that keep to these rules, and one draw needn't show every extreme that they name: For each row block f, partner[:, f] pairs the groups: partner[g, f] != g and partner[partner[g, f], f] = g.
All inputs are finite; a program needn't handle non-finite values.
Results may differ from a plain program's by a relative error of at most 0.005.
Values may be sent and summed in bfloat16 or wider, within the bound.
No kernel may reach another device: no remote copies, remote signals or barrier semaphores. Data moves between devices by JAX's collectives and lax.ppermute only.
A program may use at most 64 MiB of HBM per device.

v0:
```python
import math

import jax
import jax.numpy as jnp
from jax import lax
from jax.sharding import PartitionSpec as P

D = 4608


beta_one = 0.9
beta_two = 0.95
adam_eps = 1e-08
inner_rate = 0.1
decay_rate = 0.1
bias_one = 1.0 - (0.9**50) ** 2
bias_two = 1.0 - (0.95**50) ** 2
outer_rate = 0.7
outer_beta = 0.9


def shards(weight, momentum, adam_mean, adam_var, inputs, targets, states, partner):
    scale = 1.0 / math.sqrt(D)
    weight_loc = weight[0]
    inputs_loc = inputs[0]
    states_loc = states[0]
    mates_col = partner[:, 0]
    tokens_all = inputs_loc.shape[0] * lax.axis_size("fsdp")
    columns = inputs_loc
    pred = (
        jnp.dot(
            columns,
            lax.all_gather(weight_loc.astype(jnp.bfloat16), "fsdp", axis=0, tiled=True),
            preferred_element_type=jnp.float32,
        )
        * scale
    )
    resid = ((pred - targets[0].astype(jnp.float32)) / tokens_all).astype(jnp.bfloat16)
    columns = inputs_loc
    grad = (
        lax.psum_scatter(
            lax.dot_general(
                columns, resid, (((0,), (0,)), ((), ())), preferred_element_type=jnp.float32
            ).astype(jnp.bfloat16),
            "fsdp",
            scatter_dimension=0,
            tiled=True,
        ).astype(jnp.float32)
        * scale
    )
    mean_new = beta_one * adam_mean[0] + (1.0 - beta_one) * grad
    var_new = beta_two * adam_var[0] + (1.0 - beta_two) * grad * grad
    update = (
        mean_new / bias_one / (jnp.sqrt(var_new / bias_two) + adam_eps) + decay_rate * weight_loc
    )
    delta = inner_rate * update
    every = lax.all_gather(delta[None].astype(jnp.bfloat16), "grp", axis=0, tiled=True).astype(
        jnp.float32
    )
    mate = mates_col[lax.axis_index("grp")]
    partner_delta = lax.dynamic_index_in_dim(every, mate, 0, keepdims=False)
    average = 0.5 * (delta + partner_delta)
    new_momentum = outer_beta * momentum[0] + average
    new_weight = weight_loc - outer_rate * (average + outer_beta * new_momentum)
    columns = states_loc
    rollout = (
        jnp.dot(
            columns,
            lax.all_gather(new_weight.astype(jnp.bfloat16), "fsdp", axis=0, tiled=True),
            preferred_element_type=jnp.float32,
        )
        * scale
    )
    return (new_weight[None], new_momentum[None], rollout.astype(jnp.bfloat16)[None])


def solution(mesh):
    return jax.shard_map(
        shards,
        mesh=mesh,
        in_specs=(
            P("grp", "fsdp", None),
            P("grp", "fsdp", None),
            P("grp", "fsdp", None),
            P("grp", "fsdp", None),
            P("grp", "fsdp", None),
            P("grp", "fsdp", None),
            P("grp", "fsdp", None),
            P(None, "fsdp"),
        ),
        out_specs=(P("grp", "fsdp", None), P("grp", "fsdp", None), P("grp", "fsdp", None)),
        check_vma=False,
    )
```

profile of v0, /device:TPU:1, one launch (start us, length us, event | category | flops | bytes accessed | tf_op | source)
XLA Modules:
  0.0 410.2 jit_solution(7349931975073530848)
XLA Ops:
  7.2 0.0 copy-start
  7.2 0.0 all-gather.5.cloned.1.call-start
  7.2 1.7 bitcast_convert_fusion
  8.9 0.0 all-gather.5.cloned.1.call-update
  9.0 0.0 reduce-scatter.4.cloned.1.call-start
  9.0 94.7 %all-gather.5.cloned.1.call-done = bf16[4608,256]{1,0:T(8,128)(2,1)} async-done(((bf16[144,256]{1,0:T(8,128)(2,1)}), bf16[4608,256]{1,0:T(8,128)(2,1)}) %all-gather.5.cloned.1.call-update) | async-done | bytes 2359312 | tf_op jit(solution)/shard_map/all_gather | solution.py:33
  103.7 0.0 copy-done
  103.7 5.8 %fusion = bf16[4608,256]{0,1:T(8,128)(2,1)} fusion(bf16[1,256,4608]{2,1,0:T(8,128)(2,1)S(1)} %copy-done, bf16[4608,256]{1,0:T(8,128)(2,1)} %all-gather.5.cloned.1.call-done, bf16[1,256,256]{2,1,0:T(8,128)(2,1)} %param.13), kind=kOutput, calls=%fused_computation.1 | convolution fusion | flops 1209466880 | bytes 7208960 | tf_op jit(solution)/shard_map/dot_general | solution.py:42
  109.5 4.3 %copy.30 = bf16[4608,256]{1,0:T(8,128)(2,1)} copy(bf16[4608,256]{0,1:T(8,128)(2,1)} %fusion) | data formatting | bytes 4718592
  113.8 0.0 copy-start.1
  113.8 0.0 copy-start.2
  113.8 0.0 copy-start.3
  113.8 0.0 copy-start.5
  113.8 0.0 copy-start.4
  113.8 0.0 reduce-scatter.4.cloned.1.call-update
  113.8 0.0 all-gather.9.cloned.1.call-start
  113.9 120.6 %reduce-scatter.4.cloned.1.call-done = bf16[144,256]{1,0:T(8,128)(2,1)} async-done(((bf16[4608,256]{1,0:T(8,128)(2,1)}), bf16[144,256]{1,0:T(8,128)(2,1)}) %reduce-scatter.4.cloned.1.call-update) | async-done | bytes 73744 | tf_op jit(solution)/shard_map/reduce_scatter | solution.py:41
  234.5 0.0 copy-done.1
  234.5 0.0 copy-done.2
  234.5 0.0 copy-done.3
  234.5 1.6 fusion.49
  236.1 0.0 all-gather.9.cloned.1.call-update
  236.2 0.0 all-gather.7.cloned.1.call-start
  236.2 0.0 copy-done.5
  236.2 0.6 constant_dynamic-slice_fusion
  238.8 64.1 %all-gather.9.cloned.1.call-done = bf16[2304,256]{1,0:T(8,128)(2,1)} async-done(((bf16[144,256]{1,0:T(8,128)(2,1)}), bf16[2304,256]{1,0:T(8,128)(2,1)}) %all-gather.9.cloned.1.call-update) | async-done | bytes 1179664 | tf_op jit(solution)/shard_map/all_gather | solution.py:57
  302.8 0.0 copy-done.4
  302.8 1.7 fusion.48
  304.5 0.0 all-gather.7.cloned.1.call-update
  304.5 95.6 %all-gather.7.cloned.1.call-done = bf16[4608,256]{1,0:T(8,128)(2,1)} async-done(((bf16[144,256]{1,0:T(8,128)(2,1)}), bf16[4608,256]{1,0:T(8,128)(2,1)}) %all-gather.7.cloned.1.call-update) | async-done | bytes 2359312 | tf_op jit(solution)/shard_map/all_gather | solution.py:69
  400.1 2.8 fusion.26
  402.9 0.7 copy.29
Async XLA Ops:
  7.2 96.5 %copy-start = (bf16[1,256,4608]{2,1,0:T(8,128)(2,1)S(1)}, bf16[1,256,4608]{2,1,0:T(8,128)(2,1)}, u32[]{:S(2)}) copy-start(bf16[1,256,4608]{2,1,0:T(8,128)(2,1)} %param.12) | copy-start | bytes 7077892
  7.2 96.5 %all-gather.5.cloned.1.call-start = ((), (), s32[]{:S(2)}) async-start(), calls=%async_computation.1 | async-start | bytes 2433024 | tf_op jit(solution)/shard_map/all_gather | solution.py:33
  9.0 225.5 %reduce-scatter.4.cloned.1.call-start = ((), (), s32[]{:S(2)}) async-start(), calls=%async_computation.4 | async-start | bytes 2433024 | tf_op jit(solution)/shard_map/reduce_scatter | solution.py:41
  113.8 120.7 %copy-start.1 = (f32[1,144,256]{2,1,0:T(8,128)S(1)}, f32[1,144,256]{2,1,0:T(8,128)}, u32[]{:S(2)}) copy-start(f32[1,144,256]{2,1,0:T(8,128)} %param.8) | copy-start | bytes 442372
  113.8 120.7 %copy-start.2 = (f32[1,144,256]{2,1,0:T(8,128)S(1)}, f32[1,144,256]{2,1,0:T(8,128)}, u32[]{:S(2)}) copy-start(f32[1,144,256]{2,1,0:T(8,128)} %param.11) | copy-start | bytes 442372
  113.8 120.7 %copy-start.3 = (f32[1,144,256]{2,1,0:T(8,128)S(1)}, f32[1,144,256]{2,1,0:T(8,128)}, u32[]{:S(2)}) copy-start(f32[1,144,256]{2,1,0:T(8,128)} %param.10) | copy-start | bytes 442372
  113.8 122.4 %copy-start.5 = (s32[16,1]{0,1:T(1,128)S(1)}, s32[16,1]{0,1:T(1,128)}, u32[]{:S(2)}) copy-start(s32[16,1]{0,1:T(1,128)} %param.15) | copy-start | bytes 196
  113.8 189.0 %copy-start.4 = (f32[1,144,256]{2,1,0:T(8,128)S(1)}, f32[1,144,256]{2,1,0:T(8,128)}, u32[]{:S(2)}) copy-start(f32[1,144,256]{2,1,0:T(8,128)} %param.9) | copy-start | bytes 442372
  113.8 189.0 %all-gather.9.cloned.1.call-start = ((), (), s32[]{:S(2)}) async-start(), calls=%async_computation.3 | async-start | bytes 1253376 | tf_op jit(solution)/shard_map/all_gather | solution.py:57
  236.2 163.9 %all-gather.7.cloned.1.call-start = ((), (), s32[]{:S(2)}) async-start(), calls=%async_computation.2 | async-start | bytes 2433024 | tf_op jit(solution)/shard_map/all_gather | solution.py:69
Sparse Core Ops, SparseCore 0:
  11.9 91.7 all-gather.4
  114.0 120.4 reduce-scatter.3
  237.1 65.6 all-gather.8
  306.0 93.9 all-gather.6
where the time goes:
time: 410 us
  waiting for transfers between devices  375 us (91%)
  between operations  15.8 us (4%)
  matrix products  8.65 us (2%)
  local copies, waits for them, and re-layouts  5.63 us (1%)
  other arithmetic  5.02 us (1%)
    reduce_scatter x1, waiting for transfers between devices, shards(): lax.psum_scatter(lax.dot_general(columns, resid, (((0,), (0,)), ((), ()))...  121 us
    all_gather x1, waiting for transfers between devices, shards(): lax.all_gather(new_weight.astype(jnp.bfloat16), 'fsdp', axis=0, tiled=True)  95.6 us
    all_gather x1, waiting for transfers between devices, shards(): lax.all_gather(weight_loc.astype(jnp.bfloat16), 'fsdp', axis=0, tiled=True)  94.7 us
    all_gather x1, waiting for transfers between devices, shards(): lax.all_gather(delta[None].astype(jnp.bfloat16), 'grp', axis=0, tiled=True)  64.1 us
  transfers between devices with their start and end apart: 4, of which 4 were waited for; matrix products, arithmetic and copies ran while one was open for 0% of the time, Pallas kernels for 0%

commit v1 on v0

v1 whole, which is shorter than its diff:
```python
import math

import jax
import jax.numpy as jnp
from jax import lax
from jax.sharding import Mesh
from jax.sharding import PartitionSpec as P

D = 4608

beta_one = 0.9
beta_two = 0.95
adam_eps = 1e-08
inner_rate = 0.1
decay_rate = 0.1
bias_one = 1.0 - (0.9**50) ** 2
bias_two = 1.0 - (0.95**50) ** 2
outer_rate = 0.7
outer_beta = 0.9

GRP = ("xl", "z")
CHIPS = ("y", "xh")
SWAP = [(0, 1), (1, 0)]


def spread_all(block, axes, n):
    return lax.all_to_all(jnp.broadcast_to(block[None], (n,) + block.shape), axes, 0, 0)


def by_core(mine, other):
    core = lax.axis_index("c")
    return jnp.stack([jnp.where(core == 0, mine, other), jnp.where(core == 0, other, mine)], axis=1)


def gather_rows(block, chips):
    mine = spread_all(block, CHIPS, chips)
    other = lax.ppermute(mine, "c", SWAP)
    return by_core(mine, other).reshape(-1, block.shape[1])


def shards(weight, momentum, adam_mean, adam_var, inputs, targets, states, partner):
    scale = 1.0 / math.sqrt(D)
    chips = lax.axis_size("y") * lax.axis_size("xh")
    groups = lax.axis_size("xl") * lax.axis_size("z")
    core = lax.axis_index("c")
    weight_loc = weight[0]
    rows, width = weight_loc.shape
    inputs_loc = inputs[0]
    tokens_all = inputs_loc.shape[0] * chips * 2
    full = gather_rows(weight_loc.astype(jnp.bfloat16), chips)
    pred = jnp.dot(inputs_loc, full, preferred_element_type=jnp.float32) * scale
    resid = ((pred - targets[0].astype(jnp.float32)) / tokens_all).astype(jnp.bfloat16)
    part = lax.dot_general(
        inputs_loc, resid, (((0,), (0,)), ((), ())), preferred_element_type=jnp.float32
    ).reshape(chips, 2, rows, width)
    keep = jnp.where(core == 0, part[:, 0], part[:, 1])
    send = jnp.where(core == 0, part[:, 1], part[:, 0]).astype(jnp.bfloat16)
    both = (keep + lax.ppermute(send, "c", SWAP).astype(jnp.float32)).astype(jnp.bfloat16)
    pieces = lax.all_to_all(both, CHIPS, 0, 0)
    grad = jnp.sum(pieces.astype(jnp.float32), axis=0) * scale
    mean_new = beta_one * adam_mean[0] + (1.0 - beta_one) * grad
    var_new = beta_two * adam_var[0] + (1.0 - beta_two) * grad * grad
    update = (
        mean_new / bias_one / (jnp.sqrt(var_new / bias_two) + adam_eps) + decay_rate * weight_loc
    )
    delta = inner_rate * update
    every = spread_all(delta.astype(jnp.bfloat16), GRP, groups)
    mate = partner[:, 0][lax.axis_index(GRP)]
    partner_delta = lax.dynamic_index_in_dim(every, mate, 0, keepdims=False).astype(jnp.float32)
    average = 0.5 * (delta + partner_delta)
    new_momentum = outer_beta * momentum[0] + average
    new_weight = weight_loc - outer_rate * (average + outer_beta * new_momentum)
    full = gather_rows(new_weight.astype(jnp.bfloat16), chips)
    rollout = jnp.dot(states[0], full, preferred_element_type=jnp.float32) * scale
    return (new_weight[None], new_momentum[None], rollout.astype(jnp.bfloat16)[None])


def solution(mesh):
    fine = Mesh(mesh.devices.reshape(2, 8, 8, 2, 2), ("xl", "z", "y", "xh", "c"))
    grp, fsdp = ("xl", "z"), ("y", "xh", "c")
    row = P(grp, fsdp, None)
    return jax.shard_map(
        shards,
        mesh=fine,
        in_specs=(row, row, row, row, row, row, row, P(None, fsdp)),
        out_specs=(row, row, row),
        check_vma=False,
    )
```

time: 410 us -> 203 us (0.50)
  waiting for transfers between devices: 375 us -> 32.1 us
  blocking collectives: 0 us -> 112 us
  starting transfers between devices: 0.16 us -> 22.8 us
  between operations: 15.8 us -> 2.71 us
  other arithmetic: 5.02 us -> 12.7 us
  local copies, waits for them, and re-layouts: 5.63 us -> 11.7 us
    all_gather x3 -> x0, waiting for transfers between devices: 254 us -> none  [the longest x1 95.6 us: shards(): lax.all_gather(new_weight.astype(jnp.bfloat16), 'fsdp', axis=0, tiled=True)]
    reduce_scatter x1 -> x0, waiting for transfers between devices: 121 us -> none  [shards(): lax.psum_scatter(lax.dot_general(columns, resid, (((0,), (0,)), ((), ()))...]
    all_to_all x0 -> x3, blocking collectives: none -> 112 us  [the longest x2 77 us: spread_all(): lax.all_to_all(jnp.broadcast_to(block[None], (n,) + block.shape), axes, 0...]
    all_to_all x0 -> x1, waiting for transfers between devices: none -> 24.7 us  [spread_all(): lax.all_to_all(jnp.broadcast_to(block[None], (n,) + block.shape), axes, 0...]
    ppermute x0 -> x3, starting transfers between devices: none -> 12.5 us  [the longest x2 10.3 us: gather_rows(): other = lax.ppermute(mine, 'c', SWAP)]
    all_to_all x0 -> x1, starting transfers between devices: none -> 10.3 us  [spread_all(): lax.all_to_all(jnp.broadcast_to(block[None], (n,) + block.shape), axes, 0...]
    ppermute x0 -> x3, waiting for transfers between devices: none -> 7.48 us  [the longest x2 5.03 us: gather_rows(): other = lax.ppermute(mine, 'c', SWAP)]
    dot_general x0 -> x1, local copies, waits for them, and re-layouts: none -> 6.15 us  [shards(): lax.dot_general(inputs_loc, resid, (((0,), (0,)), ((), ())), preferred_el...]
where the time goes in v1:
time: 203 us; the launch traced here: 202 us
  blocking collectives  112 us (55%)
  waiting for transfers between devices  32.1 us (16%)
  starting transfers between devices  22.8 us (11%)
  other arithmetic  12.7 us (6%)
  local copies, waits for them, and re-layouts  11.7 us (6%)
  matrix products  7.99 us (4%)
  between operations  2.71 us (1%)
    all_to_all x2, blocking collectives, spread_all(): lax.all_to_all(jnp.broadcast_to(block[None], (n,) + block.shape), axes, 0...  77 us
    all_to_all x1, blocking collectives, shards(): pieces = lax.all_to_all(both, CHIPS, 0, 0)  35.4 us
    all_to_all x1, waiting for transfers between devices, spread_all(): lax.all_to_all(jnp.broadcast_to(block[None], (n,) + block.shape), axes, 0...  24.7 us
    all_to_all x1, starting transfers between devices, spread_all(): lax.all_to_all(jnp.broadcast_to(block[None], (n,) + block.shape), axes, 0...  10.3 us
    ppermute x2, starting transfers between devices, gather_rows(): other = lax.ppermute(mine, 'c', SWAP)  10.3 us
    dot_general x1, matrix products, shards(): lax.dot_general(inputs_loc, resid, (((0,), (0,)), ((), ())), preferred_el...  6.54 us
    dot_general x1, local copies, waits for them, and re-layouts, shards(): lax.dot_general(inputs_loc, resid, (((0,), (0,)), ((), ())), preferred_el...  6.15 us
    ppermute x2, waiting for transfers between devices, gather_rows(): other = lax.ppermute(mine, 'c', SWAP)  5.03 us
  transfers between devices with their start and end apart: 4, of which 4 were waited for; matrix products, arithmetic and copies ran while one was open for 0% of the time, Pallas kernels for 0%

profile of v1, /device:TPU:1, one launch (start us, length us, event | category | flops | bytes accessed | tf_op | source)
XLA Modules:
  0.0 202.5 jit_solution(5228288193936205185)
XLA Ops:
  0.6 1.1 convert_bitcast_fusion.2
  1.7 0.1 broadcast_in_dim.30
  1.8 42.4 %all_to_all.20 = bf16[16,144,256]{2,1,0:T(8,128)(2,1)S(1)} all-to-all(bf16[16,144,256]{2,1,0:T(8,128)(2,1)S(1)} %broadcast_in_dim.30), channel_id=1, replica_groups=mesh['xl'=2,'z'=8,'y'=8,'xh'=2,'c'=2] {'y','xh'}, dimensions={0} | all-to-all | bytes 2359296 | tf_op jit(solution)/shard_map/all_to_all | solution.py:27
  44.2 4.1 %collective-permute-start = (bf16[16,144,256]{2,1,0:T(8,128)(2,1)S(1)}, bf16[16,144,256]{2,1,0:T(8,128)(2,1)}, u32[]{:S(2)}, u32[]{:S(2)}) collective-permute-start(bf16[16,144,256]{2,1,0:T(8,128)(2,1)S(1)} %all_to_all.20), channel_id=1, source_target_pairs={{0,1},{1,0},{2,3},{3,2},{4,5},{5,4},{6,7},{7,6},{8,9},{9,8},{10,11... | collective-permute-start | bytes 3538952 | tf_op jit(solution)/shard_map/ppermute | solution.py:37
  48.3 2.6 %collective-permute-done = bf16[16,144,256]{2,1,0:T(8,128)(2,1)} collective-permute-done((bf16[16,144,256]{2,1,0:T(8,128)(2,1)S(1)}, bf16[16,144,256]{2,1,0:T(8,128)(2,1)}, u32[]{:S(2)}, u32[]{:S(2)}) %collective-permute-start) | collective-permute-done | bytes 1179680 | tf_op jit(solution)/shard_map/ppermute | solution.py:37
  50.8 1.4 select_bitcast_fusion.3
  52.3 1.7 pad_maximum_fusion
  53.9 6.5 %convolution_bitcast_fusion = f32[4608,256]{0,1:T(8,128)} fusion(bf16[1,256,4608]{2,1,0:T(8,128)(2,1)S(1)} %copy-done, bf16[4608,256]{1,0:T(8,128)(2,1)} %bitcast.101, bf16[1,256,256]{2,1,0:T(8,128)(2,1)S(1)} %copy-done.5), kind=kOutput, calls=%fused_computation | convolution fusion | flops 1208287232 | bytes 9568256 | tf_op jit(solution)/shard_map/dot_general | solution.py:53
  60.5 6.2 %copy.17 = f32[4608,256]{1,0:T(8,128)} copy(f32[4608,256]{0,1:T(8,128)} %convolution_bitcast_fusion) | data formatting | bytes 9437184 | tf_op jit(solution)/shard_map/dot_general | solution.py:53
  66.6 2.6 %fusion.4 = bf16[16,144,256]{2,1,0:T(8,128)(2,1)S(1)} fusion(f32[16,2,144,256]{3,2,1,0:T(8,128)} %bitcast.98, pred[]{:T(512)S(6)} %eq.2), kind=kLoop, calls=%fused_computation.10 | loop fusion | flops 589824 | bytes 3538945 | tf_op jit(solution)/shard_map/convert_element_type | solution.py:57
  69.2 2.3 %collective-permute-start.1 = (bf16[16,144,256]{2,1,0:T(8,128)(2,1)S(1)}, bf16[16,144,256]{2,1,0:T(8,128)(2,1)S(1)}, u32[]{:S(2)}, u32[]{:S(2)}) collective-permute-start(bf16[16,144,256]{2,1,0:T(8,128)(2,1)S(1)} %fusion.4), channel_id=1, source_target_pairs={{0,1},{1,0},{2,3},{3,2},{4,5},{5,4},{6,7},{7,6},{8,9},{9,8},{10,11... | collective-permute-start | bytes 3538952 | tf_op jit(solution)/shard_map/ppermute | solution.py:58
  71.5 2.5 %collective-permute-done.1 = bf16[16,144,256]{2,1,0:T(8,128)(2,1)S(1)} collective-permute-done((bf16[16,144,256]{2,1,0:T(8,128)(2,1)S(1)}, bf16[16,144,256]{2,1,0:T(8,128)(2,1)S(1)}, u32[]{:S(2)}, u32[]{:S(2)}) %collective-permute-start.1) | collective-permute-done | bytes 1179680 | tf_op jit(solution)/shard_map/ppermute | solution.py:58
  74.0 2.8 %fusion = bf16[16,144,256]{2,1,0:T(8,128)(2,1)S(1)} fusion(bf16[16,144,256]{2,1,0:T(8,128)(2,1)S(1)} %collective-permute-done.1, f32[16,2,144,256]{3,2,1,0:T(8,128)} %bitcast.99, pred[]{:T(512)S(6)} %eq.2), kind=kLoop, calls=%fused_computation.4 | loop fusion | flops 2359296 | bytes 7077889 | tf_op jit(solution)/shard_map/convert_element_type | solution.py:58
  76.8 35.4 %all_to_all.21 = bf16[16,144,256]{2,1,0:T(8,128)(2,1)S(1)} all-to-all(bf16[16,144,256]{2,1,0:T(8,128)(2,1)S(1)} %fusion), channel_id=1, replica_groups=mesh['xl'=2,'z'=8,'y'=8,'xh'=2,'c'=2] {'y','xh'}, dimensions={0} | all-to-all | bytes 2359296 | tf_op jit(solution)/shard_map/all_to_all | solution.py:59
  112.2 0.2 convert_reduce_fusion
  112.3 0.7 copy-done.1
  113.2 0.8 convert_bitcast_fusion.1
  114.0 1.1 broadcast_in_dim.32
  115.1 10.3 %all-to-all-start.2 = ((bf16[16,144,256]{2,1,0:T(8,128)(2,1)}), bf16[16,144,256]{2,1,0:T(8,128)(2,1)S(1)}, u32[]{:S(2)}, u32[]{:S(2)}) async-start(bf16[16,144,256]{2,1,0:T(8,128)(2,1)} %broadcast_in_dim.32), calls=%async_computation.2 | async-start | bytes 2359296 | tf_op jit(solution)/shard_map/all_to_all | solution.py:27
  125.5 0.6 constant_dynamic-slice_fusion
  128.0 24.7 %all-to-all-done.2 = bf16[16,144,256]{2,1,0:T(8,128)(2,1)S(1)} async-done(((bf16[16,144,256]{2,1,0:T(8,128)(2,1)}), bf16[16,144,256]{2,1,0:T(8,128)(2,1)S(1)}, u32[]{:S(2)}, u32[]{:S(2)}) %all-to-all-start.2) | async-done | bytes 1179680 | tf_op jit(solution)/shard_map/all_to_all | solution.py:27
  152.6 1.8 convert_bitcast_fusion
  154.5 0.1 broadcast_in_dim.34
  154.5 34.6 %all_to_all.22 = bf16[16,144,256]{2,1,0:T(8,128)(2,1)S(1)} all-to-all(bf16[16,144,256]{2,1,0:T(8,128)(2,1)S(1)} %broadcast_in_dim.34), channel_id=1, replica_groups=mesh['xl'=2,'z'=8,'y'=8,'xh'=2,'c'=2] {'y','xh'}, dimensions={0} | all-to-all | bytes 2359296 | tf_op jit(solution)/shard_map/all_to_all | solution.py:27
  189.2 6.2 %collective-permute-start.2 = (bf16[16,144,256]{2,1,0:T(8,128)(2,1)S(1)}, bf16[16,144,256]{2,1,0:T(8,128)(2,1)S(1)}, u32[]{:S(2)}, u32[]{:S(2)}) collective-permute-start(bf16[16,144,256]{2,1,0:T(8,128)(2,1)S(1)} %all_to_all.22), channel_id=1, source_target_pairs={{0,1},{1,0},{2,3},{3,2},{4,5},{5,4},{6,7},{7,6},{8,9},{9,8},{10,11... | collective-permute-start | bytes 3538952 | tf_op jit(solution)/shard_map/ppermute | solution.py:37
  195.3 2.5 %collective-permute-done.2 = bf16[16,144,256]{2,1,0:T(8,128)(2,1)S(1)} collective-permute-done((bf16[16,144,256]{2,1,0:T(8,128)(2,1)S(1)}, bf16[16,144,256]{2,1,0:T(8,128)(2,1)S(1)}, u32[]{:S(2)}, u32[]{:S(2)}) %collective-permute-start.2) | collective-permute-done | bytes 1179680 | tf_op jit(solution)/shard_map/ppermute | solution.py:37
  197.8 0.2 select_bitcast_fusion.1
  198.0 0.2 pad_maximum_fusion.1
  198.2 0.2 copy.18
  198.4 1.0 copy-done.2
  199.5 1.4 fusion.30
  200.9 1.6 copy.19
  (12 shorter events, 0.2 us)
Async XLA Ops:
  0.6 53.3 %copy-start = (bf16[1,256,4608]{2,1,0:T(8,128)(2,1)S(1)}, bf16[1,256,4608]{2,1,0:T(8,128)(2,1)}, u32[]{:S(2)}) copy-start(bf16[1,256,4608]{2,1,0:T(8,128)(2,1)} %param.12) | copy-start | bytes 7077892
  44.2 6.7 %collective-permute-start = (bf16[16,144,256]{2,1,0:T(8,128)(2,1)S(1)}, bf16[16,144,256]{2,1,0:T(8,128)(2,1)}, u32[]{:S(2)}, u32[]{:S(2)}) collective-permute-start(bf16[16,144,256]{2,1,0:T(8,128)(2,1)S(1)} %all_to_all.20), channel_id=1, source_target_pairs={{0,1},{1,0},{2,3},{3,2},{4,5},{5,4},{6,7},{7,6},{8,9},{9,8},{10,11... | collective-permute-start | bytes 3538952 | tf_op jit(solution)/shard_map/ppermute | solution.py:37
  52.3 1.7 copy-start.5
  69.2 4.7 %collective-permute-start.1 = (bf16[16,144,256]{2,1,0:T(8,128)(2,1)S(1)}, bf16[16,144,256]{2,1,0:T(8,128)(2,1)S(1)}, u32[]{:S(2)}, u32[]{:S(2)}) collective-permute-start(bf16[16,144,256]{2,1,0:T(8,128)(2,1)S(1)} %fusion.4), channel_id=1, source_target_pairs={{0,1},{1,0},{2,3},{3,2},{4,5},{5,4},{6,7},{7,6},{8,9},{9,8},{10,11... | collective-permute-start | bytes 3538952 | tf_op jit(solution)/shard_map/ppermute | solution.py:58
  112.2 0.9 copy-start.1
  112.2 1.0 copy-start.3
  112.2 1.0 copy-start.4
  115.1 10.3 %copy-start.6 = (s32[16,1]{0,1:T(1,128)S(1)}, s32[16,1]{0,1:T(1,128)}, u32[]{:S(2)}) copy-start(s32[16,1]{0,1:T(1,128)} %param.15) | copy-start | bytes 196
  115.1 37.5 %all-to-all-start.2 = ((bf16[16,144,256]{2,1,0:T(8,128)(2,1)}), bf16[16,144,256]{2,1,0:T(8,128)(2,1)S(1)}, u32[]{:S(2)}, u32[]{:S(2)}) async-start(bf16[16,144,256]{2,1,0:T(8,128)(2,1)} %broadcast_in_dim.32), calls=%async_computation.2 | async-start | bytes 2359296 | tf_op jit(solution)/shard_map/all_to_all | solution.py:27
  189.2 8.6 %collective-permute-start.2 = (bf16[16,144,256]{2,1,0:T(8,128)(2,1)S(1)}, bf16[16,144,256]{2,1,0:T(8,128)(2,1)S(1)}, u32[]{:S(2)}, u32[]{:S(2)}) collective-permute-start(bf16[16,144,256]{2,1,0:T(8,128)(2,1)S(1)} %all_to_all.22), channel_id=1, source_target_pairs={{0,1},{1,0},{2,3},{3,2},{4,5},{5,4},{6,7},{7,6},{8,9},{9,8},{10,11... | collective-permute-start | bytes 3538952 | tf_op jit(solution)/shard_map/ppermute | solution.py:37
  198.2 1.3 copy-start.2

commit v2 on v1

v2 whole, which is shorter than its diff:
```python
import functools
import math

import jax
import jax.numpy as jnp
from jax import lax
from jax.experimental import pallas as pl
from jax.experimental.pallas import tpu as pltpu
from jax.sharding import Mesh
from jax.sharding import PartitionSpec as P

D = 4608

beta_one = 0.9
beta_two = 0.95
adam_eps = 1e-08
inner_rate = 0.1
decay_rate = 0.1
bias_one = 1.0 - (0.9**50) ** 2
bias_two = 1.0 - (0.95**50) ** 2
outer_rate = 0.7
outer_beta = 0.9
scale = 1.0 / math.sqrt(D)

f32, bf16 = jnp.float32, jnp.bfloat16

AXES = (("xl", 2), ("z", 8), ("yh", 4), ("yl", 2), ("xh", 2), ("c", 2))
GRP = ("xl", "z")
FSDP = ("yh", "yl", "xh", "c")
FAR = ("yh",)
NEAR = ("yl", "xh")
NFAR, NNEAR = 4, 4
GROUPS = 16
SUB = 16
SWAP = [(0, 1), (1, 0)]

VMEM = pl.BlockSpec(memory_space=pltpu.MemorySpace.VMEM)
SMEM = pl.BlockSpec(memory_space=pltpu.MemorySpace.SMEM)


def block_rows(far, near, core, rows):
    start = rows * (2 * NNEAR * far + 2 * near) + rows * core
    return pl.ds(pl.multiple_of(start, 16), rows)


def pred_kernel(mine_ref, other_ref, weight_ref, target_ref, out_ref, full_ref):
    core = lax.axis_index("c")
    rows = weight_ref.shape[2]
    for far in range(NFAR):
        for near in range(NNEAR):
            full_ref[block_rows(far, near, core, rows), :] = weight_ref[near, far]
            full_ref[block_rows(far, near, 1 - core, rows), :] = jnp.zeros_like(weight_ref[near, far])
    mine = jnp.dot(mine_ref[...], full_ref[...], preferred_element_type=f32)
    out_ref[0] = mine * scale - target_ref[...].astype(f32)
    other = jnp.dot(other_ref[...], full_ref[...], preferred_element_type=f32)
    out_ref[1] = other * scale


def grad_kernel(tokens, mine_ref, other_ref, here_ref, there_ref, out_ref, part_ref):
    core = lax.axis_index("c")
    rows = out_ref.shape[2]
    resid_mine = ((here_ref[0] + there_ref[1]) / tokens).astype(bf16)
    resid_other = ((here_ref[1] + there_ref[0]) / tokens).astype(bf16)
    dims = (((0,), (0,)), ((), ()))
    span = 2 * NNEAR * rows
    for far in range(NFAR):
        cols = pl.ds(far * span, span)
        part_ref[far] = lax.dot_general(
            mine_ref[:, cols], resid_mine, dims, preferred_element_type=f32
        ) + lax.dot_general(other_ref[:, cols], resid_other, dims, preferred_element_type=f32)
        for near in range(NNEAR):
            out_ref[near, far] = part_ref[far, block_rows(0, near, core, rows), :].astype(bf16)


def sum_kernel(parts_ref, out_ref):
    total = parts_ref[0].astype(f32)
    for i in range(1, NNEAR):
        total += parts_ref[i].astype(f32)
    out_ref[...] = total.astype(bf16)


def delta_kernel(parts_ref, weight_ref, mean_ref, var_ref, delta_ref, pieces_ref):
    total = parts_ref[0].astype(f32)
    for i in range(1, NFAR):
        total += parts_ref[i].astype(f32)
    grad = total * scale
    mean_new = beta_one * mean_ref[...] + (1.0 - beta_one) * grad
    var_new = beta_two * var_ref[...] + (1.0 - beta_two) * grad * grad
    update = mean_new / bias_one / (jnp.sqrt(var_new / bias_two) + adam_eps)
    delta = inner_rate * (update + decay_rate * weight_ref[...])
    delta_ref[...] = delta
    rows = delta.shape[0]
    for i in range(GROUPS):
        if (i + 1) * SUB <= rows:
            pieces_ref[i] = delta[i * SUB : (i + 1) * SUB].astype(bf16)
        else:
            pieces_ref[i] = jnp.zeros_like(pieces_ref[i])


def mates_kernel(partner_ref, pieces_ref, out_ref):
    for g in range(GROUPS):
        out_ref[g] = pieces_ref[partner_ref[g]]


def update_kernel(pieces_ref, delta_ref, weight_ref, momentum_ref, new_w_ref, new_m_ref, send_ref):
    rows = delta_ref.shape[0]
    for i in range(rows // SUB):
        at = slice(i * SUB, (i + 1) * SUB)
        average = 0.5 * (delta_ref[at] + pieces_ref[i].astype(f32))
        new_momentum = outer_beta * momentum_ref[at] + average
        new_weight = weight_ref[at] - outer_rate * (average + outer_beta * new_momentum)
        new_m_ref[at] = new_momentum
        new_w_ref[at] = new_weight
        for j in range(NFAR):
            send_ref[j, at] = new_weight.astype(bf16)


def cast_kernel(weight_ref, send_ref):
    for j in range(NFAR):
        send_ref[j] = weight_ref[...].astype(bf16)


def rollout_kernel(states_ref, mine_ref, other_ref, out_ref, full_ref):
    core = lax.axis_index("c")
    rows = mine_ref.shape[2]
    for far in range(NFAR):
        for near in range(NNEAR):
            full_ref[block_rows(far, near, core, rows), :] = mine_ref[near, far]
            full_ref[block_rows(far, near, 1 - core, rows), :] = other_ref[near, far]
    out = jnp.dot(states_ref[...], full_ref[...], preferred_element_type=f32) * scale
    out_ref[...] = out.astype(bf16)


def call(kernel, out, ins, scratch=(), name=None, mib=6):
    run = pl.pallas_call(
        kernel,
        out_shape=out,
        in_specs=[SMEM if space == "s" else VMEM for space in ins],
        out_specs=jax.tree.map(lambda _: VMEM, out),
        scratch_shapes=scratch,
        compiler_params=pltpu.CompilerParams(vmem_limit_bytes=mib << 20),
        name=name,
    )

    def apply(*args):
        held = [
            pltpu.with_memory_space_constraint(a, pltpu.MemorySpace.VMEM) if space == "v" else a
            for a, space in zip(args, ins)
        ]
        return run(*held)

    return apply


def gather_rows(send):
    far = lax.all_to_all(send, FAR, 0, 0)
    return lax.all_to_all(jnp.broadcast_to(far[None], (NNEAR,) + far.shape), NEAR, 0, 0)


def shards(weight, momentum, adam_mean, adam_var, inputs, targets, states, partner):
    weight, momentum, adam_mean, adam_var = weight[0], momentum[0], adam_mean[0], adam_var[0]
    inputs, targets, states, partner = inputs[0], targets[0], states[0], partner[:, 0]
    rows, width = weight.shape
    count, depth = inputs.shape
    tokens_all = count * NFAR * NNEAR * 2
    S = jax.ShapeDtypeStruct
    V = pltpu.VMEM

    inputs_other = lax.ppermute(inputs, "c", SWAP)
    send = call(cast_kernel, V((NFAR, rows, width), bf16), "h", name="cast")(weight)
    parts = gather_rows(send)
    here = call(
        pred_kernel, V((2, count, width), f32), "vvvv", [pltpu.VMEM((depth, width), bf16)], "pred", 16
    )(inputs, inputs_other, parts, targets)
    there = lax.ppermute(here, "c", SWAP)
    grads = call(
        functools.partial(grad_kernel, tokens_all),
        V((NNEAR, NFAR, rows, width), bf16),
        "vvvv",
        [pltpu.VMEM((NFAR, 2 * NNEAR * rows, width), f32)],
        "grad",
        20,
    )(inputs, inputs_other, here, there)
    near = lax.all_to_all(grads, NEAR, 0, 0)
    near = call(sum_kernel, V((NFAR, rows, width), bf16), "v", name="near_sum")(near)
    far = lax.all_to_all(near, FAR, 0, 0)
    piece = V((GROUPS, SUB, width), bf16)
    delta, pieces = call(delta_kernel, (V((rows, width), f32), piece), "vvvv", name="delta")(
        far, weight, adam_mean, adam_var
    )
    pieces = lax.all_to_all(pieces, GRP, 0, 0)
    pieces = call(mates_kernel, piece, "sv", name="mates")(partner, pieces)
    pieces = lax.all_to_all(pieces, GRP, 0, 0)
    new_weight, new_momentum, send = call(
        update_kernel,
        (S((rows, width), f32), S((rows, width), f32), V((NFAR, rows, width), bf16)),
        "vvvv",
        name="update",
    )(pieces, delta, weight, momentum)
    mine = gather_rows(send)
    other = lax.ppermute(mine, "c", SWAP)
    rollout = call(
        rollout_kernel,
        S((states.shape[0], width), bf16),
        "vvv",
        [pltpu.VMEM((depth, width), bf16)],
        "rollout",
        12,
    )(states, mine, other)
    return new_weight[None], new_momentum[None], rollout[None]


def solution(mesh):
    names = tuple(name for name, _ in AXES)
    fine = Mesh(mesh.devices.reshape(tuple(size for _, size in AXES)), names)
    row = P(GRP, FSDP, None)
    return jax.shard_map(
        shards,
        mesh=fine,
        in_specs=(row, row, row, row, row, row, row, P(None, FSDP)),
        out_specs=(row, row, row),
        check_vma=False,
    )
```

time: 203 us -> 154 us (0.76)
  waiting for transfers between devices: 32.1 us -> 3.97 us
  other arithmetic: 12.7 us -> 0 us
  local copies, waits for them, and re-layouts: 11.7 us -> 1.1 us
  matrix products: 7.99 us -> 0 us
  Pallas kernels: 0 us -> 6.65 us
  blocking collectives: 112 us -> 117 us
    all_to_all x1 -> x0, waiting for transfers between devices: 24.7 us -> none  [spread_all(): lax.all_to_all(jnp.broadcast_to(block[None], (n,) + block.shape), axes, 0...]
    ppermute x3, starting transfers between devices: 12.5 us -> 24.1 us  [the longest x1 9.07 us: shards(): other = lax.ppermute(mine, 'c', SWAP)]
    all_to_all x1 -> x0, starting transfers between devices: 10.3 us -> none  [spread_all(): lax.all_to_all(jnp.broadcast_to(block[None], (n,) + block.shape), axes, 0...]
    dot_general x2 -> x0, matrix products: 7.99 us -> none  [the longest x1 6.54 us: shards(): lax.dot_general(inputs_loc, resid, (((0,), (0,)), ((), ())), preferred_el...]
    pallas_call x0 -> x8, Pallas kernels: none -> 6.65 us  [apply(): return run(*held)]
    dot_general x1 -> x0, local copies, waits for them, and re-layouts: 6.15 us -> none  [shards(): lax.dot_general(inputs_loc, resid, (((0,), (0,)), ((), ())), preferred_el...]
    convert_element_type x2 -> x0, other arithmetic: 5.43 us -> none  [the longest x1 2.84 us: shards(): (keep + lax.ppermute(send, 'c', SWAP).astype(jnp.float32)).astype(jnp.bfl...]
    all_to_all x3 -> x8, blocking collectives: 112 us -> 117 us  [the longest x2 30.5 us: gather_rows(): lax.all_to_all(jnp.broadcast_to(far[None], (NNEAR,) + far.shape), NEAR, 0...]
  transfers between devices with their start and end apart: 4 -> 3, of which waited for: 4 -> 2; matrix products, arithmetic and copies ran while one was open for 0% -> 0% of each run, Pallas kernels for 0% -> 0%
where the time goes in v2:
time: 154 us; the launch traced here: 153 us
  blocking collectives  117 us (76%)
  starting transfers between devices  24.1 us (16%)
  Pallas kernels  6.65 us (4%)
  waiting for transfers between devices  3.97 us (3%)
    all_to_all x2, blocking collectives, gather_rows(): lax.all_to_all(jnp.broadcast_to(far[None], (NNEAR,) + far.shape), NEAR, 0...  30.5 us
    all_to_all x2, blocking collectives, shards(): pieces = lax.all_to_all(pieces, GRP, 0, 0)  27.6 us
    all_to_all x2, blocking collectives, gather_rows(): far = lax.all_to_all(send, FAR, 0, 0)  27.1 us
    all_to_all x1, blocking collectives, shards(): near = lax.all_to_all(grads, NEAR, 0, 0)  18.9 us
    all_to_all x1, blocking collectives, shards(): far = lax.all_to_all(near, FAR, 0, 0)  12.5 us
    ppermute x1, starting transfers between devices, shards(): other = lax.ppermute(mine, 'c', SWAP)  9.07 us
    ppermute x1, starting transfers between devices, shards(): inputs_other = lax.ppermute(inputs, 'c', SWAP)  8.75 us
    pallas_call x8, Pallas kernels, apply(): return run(*held)  6.65 us
  transfers between devices with their start and end apart: 3, of which 2 were waited for; matrix products, arithmetic and copies ran while one was open for 0% of the time, Pallas kernels for 0%

profile of v2, /device:TPU:1, one launch (start us, length us, event | category | flops | bytes accessed | tf_op | source)
XLA Modules:
  0.0 153.2 jit_solution(4888738262113120706)
XLA Ops:
  0.6 8.7 %collective-permute-start = (bf16[256,4608]{1,0:T(8,128)(2,1)}, bf16[256,4608]{1,0:T(8,128)(2,1)S(1)}, u32[]{:S(2)}, u32[]{:S(2)}) collective-permute-start(bf16[256,4608]{1,0:T(8,128)(2,1)} %bitcast.11), channel_id=1, source_target_pairs={{0,1},{1,0},{2,3},{3,2},{4,5},{5,4},{6,7},{7,6},{8,9},{9,8},{10,11... | collective-permute-start | bytes 7077896 | tf_op jit(solution)/shard_map/ppermute | solution.py:169
  9.4 0.0 copy-start.1
  9.4 0.9 copy-done.1
  10.3 13.2 %all_to_all.40 = bf16[4,144,256]{2,1,0:T(8,128)(2,1)S(1)} all-to-all(bf16[4,144,256]{2,1,0:T(8,128)(2,1)S(1)} %cast.1), channel_id=1, replica_groups=mesh['xl'=2,'z'=8,'yh'=4,'yl'=2,'xh'=2,'c'=2] {'yh'}, dimensions={0} | all-to-all | bytes 589824 | tf_op jit(solution)/shard_map/all_to_all | solution.py:156
  23.5 0.1 broadcast_in_dim.10
  23.6 0.0 copy-start
  23.6 16.2 %all_to_all.41.weight_ref = bf16[4,4,144,256]{3,2,1,0:T(8,128)(2,1)S(1)} all-to-all(bf16[4,4,144,256]{3,2,1,0:T(8,128)(2,1)S(1)} %broadcast_in_dim.10), channel_id=1, replica_groups=mesh['xl'=2,'z'=8,'yh'=4,'yl'=2,'xh'=2,'c'=2] {'yl','xh'}, dimensions={0} | all-to-all | bytes 2359296 | tf_op jit(solution)/shard_map/all_to_all | solution.py:157
  39.8 0.0 collective-permute-done.other_ref
  39.8 0.0 copy-done.7
  39.8 0.0 copy-done
  39.8 1.4 pred_.1.here_ref
  41.2 6.3 %collective-permute-start.1 = (f32[2,256,256]{2,1,0:T(8,128)S(1)}, f32[2,256,256]{2,1,0:T(8,128)S(1)}, u32[]{:S(2)}, u32[]{:S(2)}) collective-permute-start(f32[2,256,256]{2,1,0:T(8,128)S(1)} %pred_.1.here_ref), channel_id=1, source_target_pairs={{0,1},{1,0},{2,3},{3,2},{4,5},{5,4},{6,7},{7,6},{8,9},{9,8},{10,11... | collective-permute-start | bytes 1572872 | tf_op jit(solution)/shard_map/ppermute | solution.py:175
  47.5 1.5 collective-permute-done.1.there_ref
  49.1 2.1 %grad.1 = bf16[4,4,144,256]{3,2,1,0:T(8,128)(2,1)S(1)} custom-call(bf16[256,4608]{1,0:T(8,128)(2,1)S(1)} %bitcast.13, bf16[256,4608]{1,0:T(8,128)(2,1)S(1)} %collective-permute-done.other_ref, f32[2,256,256]{2,1,0:T(8,128)S(1)} %pred_.1.here_ref, f32[2,256,256]{2,1,0:T(8,128)S(1)} %collective-permute-done.1.there_ref), custom_call_target="tpu_custom_call" | custom-call | tf_op jit(solution)/shard_map/grad/pallas_call | solution.py:150
  51.2 18.9 %all_to_all.42.parts_ref = bf16[4,4,144,256]{3,2,1,0:T(8,128)(2,1)S(1)} all-to-all(bf16[4,4,144,256]{3,2,1,0:T(8,128)(2,1)S(1)} %grad.1), channel_id=1, replica_groups=mesh['xl'=2,'z'=8,'yh'=4,'yl'=2,'xh'=2,'c'=2] {'yl','xh'}, dimensions={0} | all-to-all | bytes 2359296 | tf_op jit(solution)/shard_map/all_to_all | solution.py:184
  70.1 0.1 near_sum.1
  70.2 0.0 copy-start.4
  70.2 12.5 %all_to_all.43.parts_ref = bf16[4,144,256]{2,1,0:T(8,128)(2,1)S(1)} all-to-all(bf16[4,144,256]{2,1,0:T(8,128)(2,1)S(1)} %near_sum.1), channel_id=1, replica_groups=mesh['xl'=2,'z'=8,'yh'=4,'yl'=2,'xh'=2,'c'=2] {'yh'}, dimensions={0} | all-to-all | bytes 589824 | tf_op jit(solution)/shard_map/all_to_all | solution.py:186
  82.8 0.2 delta.1
  82.9 17.4 %all_to_all.44.pieces_ref = bf16[16,16,256]{2,1,0:T(8,128)(2,1)S(1)} all-to-all(bf16[16,16,256]{2,1,0:T(8,128)(2,1)S(1)} %get-tuple-element.8), channel_id=1, replica_groups=mesh['xl'=2,'z'=8,'yh'=4,'yl'=2,'xh'=2,'c'=2] {'xl','z'}, dimensions={0} | all-to-all | bytes 262144 | tf_op jit(solution)/shard_map/all_to_all | solution.py:191
  100.3 0.0 copy-done.8
  100.3 0.6 mates.1
  100.9 10.2 %all_to_all.45.pieces_ref = bf16[16,16,256]{2,1,0:T(8,128)(2,1)S(1)} all-to-all(bf16[16,16,256]{2,1,0:T(8,128)(2,1)S(1)} %mates.1), channel_id=1, replica_groups=mesh['xl'=2,'z'=8,'yh'=4,'yl'=2,'xh'=2,'c'=2] {'xl','z'}, dimensions={0} | all-to-all | bytes 262144 | tf_op jit(solution)/shard_map/all_to_all | solution.py:193
  111.1 0.0 copy-done.4
  111.1 0.8 update.1
  111.9 13.9 %all_to_all.46 = bf16[4,144,256]{2,1,0:T(8,128)(2,1)S(1)} all-to-all(bf16[4,144,256]{2,1,0:T(8,128)(2,1)S(1)} %get-tuple-element.12), channel_id=1, replica_groups=mesh['xl'=2,'z'=8,'yh'=4,'yl'=2,'xh'=2,'c'=2] {'yh'}, dimensions={0} | all-to-all | bytes 589824 | tf_op jit(solution)/shard_map/all_to_all | solution.py:156
  125.8 0.1 broadcast_in_dim.24
  125.8 0.0 copy-start.3
  125.8 14.3 %all_to_all.47.mine_ref = bf16[4,4,144,256]{3,2,1,0:T(8,128)(2,1)S(1)} all-to-all(bf16[4,4,144,256]{3,2,1,0:T(8,128)(2,1)S(1)} %broadcast_in_dim.24), channel_id=1, replica_groups=mesh['xl'=2,'z'=8,'yh'=4,'yl'=2,'xh'=2,'c'=2] {'yl','xh'}, dimensions={0} | all-to-all | bytes 2359296 | tf_op jit(solution)/shard_map/all_to_all | solution.py:157
  140.2 9.1 %collective-permute-start.2 = (bf16[4,4,144,256]{3,2,1,0:T(8,128)(2,1)S(1)}, bf16[4,4,144,256]{3,2,1,0:T(8,128)(2,1)S(1)}, u32[]{:S(2)}, u32[]{:S(2)}) collective-permute-start(bf16[4,4,144,256]{3,2,1,0:T(8,128)(2,1)S(1)} %all_to_all.47.mine_ref), channel_id=1, source_target_pairs={{0,1},{1,0},{2,3},{3,2},{4,5},{5,4},{6,7},{7,6},{8,9},{9,8},{10,11... | collective-permute-start | bytes 3538952 | tf_op jit(solution)/shard_map/ppermute | solution.py:201
  149.3 2.5 %collective-permute-done.2.other_ref = bf16[4,4,144,256]{3,2,1,0:T(8,128)(2,1)S(1)} collective-permute-done((bf16[4,4,144,256]{3,2,1,0:T(8,128)(2,1)S(1)}, bf16[4,4,144,256]{3,2,1,0:T(8,128)(2,1)S(1)}, u32[]{:S(2)}, u32[]{:S(2)}) %collective-permute-start.2) | collective-permute-done | bytes 1179680 | tf_op jit(solution)/shard_map/ppermute | solution.py:201
  151.7 1.5 rollout.1
  (10 shorter events, 0.0 us)
Async XLA Ops:
  0.6 39.2 %collective-permute-start = (bf16[256,4608]{1,0:T(8,128)(2,1)}, bf16[256,4608]{1,0:T(8,128)(2,1)S(1)}, u32[]{:S(2)}, u32[]{:S(2)}) collective-permute-start(bf16[256,4608]{1,0:T(8,128)(2,1)} %bitcast.11), channel_id=1, source_target_pairs={{0,1},{1,0},{2,3},{3,2},{4,5},{5,4},{6,7},{7,6},{8,9},{9,8},{10,11... | collective-permute-start | bytes 7077896 | tf_op jit(solution)/shard_map/ppermute | solution.py:169
  9.4 0.9 copy-start.1
  23.5 16.3 %copy-start.7 = (bf16[1,256,256]{2,1,0:T(8,128)(2,1)S(1)}, bf16[1,256,256]{2,1,0:T(8,128)(2,1)}, u32[]{:S(2)}) copy-start(bf16[1,256,256]{2,1,0:T(8,128)(2,1)} %param.13) | copy-start | bytes 393220
  23.6 16.2 %copy-start = (bf16[1,256,4608]{2,1,0:T(8,128)(2,1)S(1)}, bf16[1,256,4608]{2,1,0:T(8,128)(2,1)}, u32[]{:S(2)}) copy-start(bf16[1,256,4608]{2,1,0:T(8,128)(2,1)} %param.12) | copy-start | bytes 7077892
  41.2 7.8 %collective-permute-start.1 = (f32[2,256,256]{2,1,0:T(8,128)S(1)}, f32[2,256,256]{2,1,0:T(8,128)S(1)}, u32[]{:S(2)}, u32[]{:S(2)}) collective-permute-start(f32[2,256,256]{2,1,0:T(8,128)S(1)} %pred_.1.here_ref), channel_id=1, source_target_pairs={{0,1},{1,0},{2,3},{3,2},{4,5},{5,4},{6,7},{7,6},{8,9},{9,8},{10,11... | collective-permute-start | bytes 1572872 | tf_op jit(solution)/shard_map/ppermute | solution.py:175
  70.1 12.7 %copy-start.2 = (f32[1,144,256]{2,1,0:T(8,128)S(1)}, f32[1,144,256]{2,1,0:T(8,128)}, u32[]{:S(2)}) copy-start(f32[1,144,256]{2,1,0:T(8,128)} %param.8) | copy-start | bytes 442372
  70.1 12.7 %copy-start.5 = (f32[1,144,256]{2,1,0:T(8,128)S(1)}, f32[1,144,256]{2,1,0:T(8,128)}, u32[]{:S(2)}) copy-start(f32[1,144,256]{2,1,0:T(8,128)} %param.10) | copy-start | bytes 442372
  70.1 12.7 %copy-start.6 = (f32[1,144,256]{2,1,0:T(8,128)S(1)}, f32[1,144,256]{2,1,0:T(8,128)}, u32[]{:S(2)}) copy-start(f32[1,144,256]{2,1,0:T(8,128)} %param.11) | copy-start | bytes 442372
  70.1 30.3 %copy-start.8 = (s32[16,1]{0,1:T(1,128)S(1)}, s32[16,1]{0,1:T(1,128)}, u32[]{:S(2)}) copy-start(s32[16,1]{0,1:T(1,128)} %param.15) | copy-start | bytes 196
  70.2 40.9 %copy-start.4 = (f32[1,144,256]{2,1,0:T(8,128)S(1)}, f32[1,144,256]{2,1,0:T(8,128)}, u32[]{:S(2)}) copy-start(f32[1,144,256]{2,1,0:T(8,128)} %param.9) | copy-start | bytes 442372
  125.8 25.9 %copy-start.3 = (bf16[1,128,4608]{2,1,0:T(8,128)(2,1)S(1)}, bf16[1,128,4608]{2,1,0:T(8,128)(2,1)}, u32[]{:S(2)}) copy-start(bf16[1,128,4608]{2,1,0:T(8,128)(2,1)} %param.14) | copy-start | bytes 3538948
  140.2 11.5 %collective-permute-start.2 = (bf16[4,4,144,256]{3,2,1,0:T(8,128)(2,1)S(1)}, bf16[4,4,144,256]{3,2,1,0:T(8,128)(2,1)S(1)}, u32[]{:S(2)}, u32[]{:S(2)}) collective-permute-start(bf16[4,4,144,256]{3,2,1,0:T(8,128)(2,1)S(1)} %all_to_all.47.mine_ref), channel_id=1, source_target_pairs={{0,1},{1,0},{2,3},{3,2},{4,5},{5,4},{6,7},{7,6},{8,9},{9,8},{10,11... | collective-permute-start | bytes 3538952 | tf_op jit(solution)/shard_map/ppermute | solution.py:201

commit v3 on v2

--- a/solution.py
+++ b/solution.py
@@ -28,7 +28,6 @@
 GRP = ("xl", "z")
 FSDP = ("yh", "yl", "xh", "c")
 FAR = ("yh",)
-NEAR = ("yl", "xh")
 NFAR, NNEAR = 4, 4
 GROUPS = 16
 SUB = 16
@@ -39,8 +38,19 @@
 
 
 def block_rows(far, near, core, rows):
-    start = rows * (2 * NNEAR * far + 2 * near) + rows * core
+    pair, xh = near // 2, near % 2
+    yl = core if pair == 0 else 1 - core
+    start = rows * (2 * NNEAR * far + 2 * xh) + rows * core + 4 * rows * yl
     return pl.ds(pl.multiple_of(start, 16), rows)
+
+
+def near_groups():
+    groups = []
+    for core in range(2):
+        for k in range(4):
+            ys = [(2 * k + core + i) % 8 for i in range(2)]
+            groups.append([(y * 2 + xh) * 2 + core for y in ys for xh in range(2)])
+    return groups
 
 
 def pred_kernel(mine_ref, other_ref, weight_ref, target_ref, out_ref, full_ref):
@@ -152,9 +162,13 @@
     return apply
 
 
+def near_exchange(x):
+    return lax.all_to_all(x, FSDP, 0, 0, axis_index_groups=near_groups())
+
+
 def gather_rows(send):
     far = lax.all_to_all(send, FAR, 0, 0)
-    return lax.all_to_all(jnp.broadcast_to(far[None], (NNEAR,) + far.shape), NEAR, 0, 0)
+    return near_exchange(jnp.broadcast_to(far[None], (NNEAR,) + far.shape))
 
 
 def shards(weight, momentum, adam_mean, adam_var, inputs, targets, states, partner):
@@ -181,7 +195,7 @@
         "grad",
         20,
     )(inputs, inputs_other, here, there)
-    near = lax.all_to_all(grads, NEAR, 0, 0)
+    near = near_exchange(grads)
     near = call(sum_kernel, V((NFAR, rows, width), bf16), "v", name="near_sum")(near)
     far = lax.all_to_all(near, FAR, 0, 0)
     piece = V((GROUPS, SUB, width), bf16)

time: 154 us -> 156 us (1.013)
  blocking collectives: 117 us -> 128 us
  starting transfers between devices: 24.1 us -> 15.8 us
    all_to_all x3, blocking collectives: 49.4 us -> 60.5 us  [near_exchange(): return lax.all_to_all(x, FSDP, 0, 0, axis_index_groups=near_groups())]
    ppermute x1, starting transfers between devices: 9.07 us -> 4.05 us  [shards(): other = lax.ppermute(mine, 'c', SWAP)]
    ppermute x1, starting transfers between devices: 6.29 us -> 3.01 us  [shards(): there = lax.ppermute(here, 'c', SWAP)]
where the time goes in v3:
time: 156 us; the launch traced here: 155 us
  blocking collectives  128 us (82%)
  starting transfers between devices  15.8 us (10%)
  Pallas kernels  6.12 us (4%)
  waiting for transfers between devices  3.97 us (3%)
    all_to_all x3, blocking collectives, near_exchange(): return lax.all_to_all(x, FSDP, 0, 0, axis_index_groups=near_groups())  60.5 us
    all_to_all x2, blocking collectives, shards(): pieces = lax.all_to_all(pieces, GRP, 0, 0)  27.9 us
    all_to_all x2, blocking collectives, gather_rows(): far = lax.all_to_all(send, FAR, 0, 0)  26.5 us
    all_to_all x1, blocking collectives, shards(): far = lax.all_to_all(near, FAR, 0, 0)  12.8 us
    ppermute x1, starting transfers between devices, shards(): inputs_other = lax.ppermute(inputs, 'c', SWAP)  8.75 us
    pallas_call x8, Pallas kernels, apply(): return run(*held)  6.12 us
    ppermute x1, starting transfers between devices, shards(): other = lax.ppermute(mine, 'c', SWAP)  4.05 us
  transfers between devices with their start and end apart: 3, of which 2 were waited for; matrix products, arithmetic and copies ran while one was open for 0% of the time, Pallas kernels for 0%

profile of v3, /device:TPU:1, one launch (start us, length us, event | category | flops | bytes accessed | tf_op | source)
XLA Modules:
  0.0 155.4 jit_solution(13498549985141188895)
XLA Ops:
  0.6 8.7 %collective-permute-start = (bf16[256,4608]{1,0:T(8,128)(2,1)}, bf16[256,4608]{1,0:T(8,128)(2,1)S(1)}, u32[]{:S(2)}, u32[]{:S(2)}) collective-permute-start(bf16[256,4608]{1,0:T(8,128)(2,1)} %bitcast.11), channel_id=1, source_target_pairs={{0,1},{1,0},{2,3},{3,2},{4,5},{5,4},{6,7},{7,6},{8,9},{9,8},{10,11... | collective-permute-start | bytes 7077896 | tf_op jit(solution)/shard_map/ppermute | solution.py:183
  9.4 0.0 copy-start.1
  9.4 0.9 copy-done.1
  10.3 13.2 %all_to_all.40 = bf16[4,144,256]{2,1,0:T(8,128)(2,1)S(1)} all-to-all(bf16[4,144,256]{2,1,0:T(8,128)(2,1)S(1)} %cast.1), channel_id=1, replica_groups=mesh['xl'=2,'z'=8,'yh'=4,'yl'=2,'xh'=2,'c'=2] {'yh'}, dimensions={0} | all-to-all | bytes 589824 | tf_op jit(solution)/shard_map/all_to_all | solution.py:170
  23.5 0.1 broadcast_in_dim.10
  23.6 0.0 copy-start
  23.6 21.0 %all_to_all.41.weight_ref = bf16[4,4,144,256]{3,2,1,0:T(8,128)(2,1)S(1)} all-to-all(bf16[4,4,144,256]{3,2,1,0:T(8,128)(2,1)S(1)} %broadcast_in_dim.10), channel_id=1, replica_groups={{0,2,4,6},{8,10,12,14},{16,18,20,22},{24,26,28,30},{5,7,9,11},{13,15,17..., dimensions={0} | all-to-all | bytes 2359296 | tf_op jit(solution)/shard_map/all_to_all | solution.py:166
  44.6 0.0 collective-permute-done.other_ref
  44.6 0.0 copy-done.7
  44.6 1.5 pred_.1.here_ref
  46.2 3.0 %collective-permute-start.1 = (f32[2,256,256]{2,1,0:T(8,128)S(1)}, f32[2,256,256]{2,1,0:T(8,128)S(1)}, u32[]{:S(2)}, u32[]{:S(2)}) collective-permute-start(f32[2,256,256]{2,1,0:T(8,128)S(1)} %pred_.1.here_ref), channel_id=1, source_target_pairs={{0,1},{1,0},{2,3},{3,2},{4,5},{5,4},{6,7},{7,6},{8,9},{9,8},{10,11... | collective-permute-start | bytes 1572872 | tf_op jit(solution)/shard_map/ppermute | solution.py:189
  49.2 1.5 collective-permute-done.1.there_ref
  50.7 1.7 %grad.1 = bf16[4,4,144,256]{3,2,1,0:T(8,128)(2,1)S(1)} custom-call(bf16[256,4608]{1,0:T(8,128)(2,1)S(1)} %bitcast.13, bf16[256,4608]{1,0:T(8,128)(2,1)S(1)} %collective-permute-done.other_ref, f32[2,256,256]{2,1,0:T(8,128)S(1)} %pred_.1.here_ref, f32[2,256,256]{2,1,0:T(8,128)S(1)} %collective-permute-done.1.there_ref), custom_call_target="tpu_custom_call" | custom-call | tf_op jit(solution)/shard_map/grad/pallas_call | solution.py:160
  52.4 20.1 %all_to_all.42.parts_ref = bf16[4,4,144,256]{3,2,1,0:T(8,128)(2,1)S(1)} all-to-all(bf16[4,4,144,256]{3,2,1,0:T(8,128)(2,1)S(1)} %grad.1), channel_id=1, replica_groups={{0,2,4,6},{8,10,12,14},{16,18,20,22},{24,26,28,30},{5,7,9,11},{13,15,17..., dimensions={0} | all-to-all | bytes 2359296 | tf_op jit(solution)/shard_map/all_to_all | solution.py:166
  72.5 0.1 near_sum.1
  72.7 0.0 copy-start.4
  72.7 12.8 %all_to_all.43.parts_ref = bf16[4,144,256]{2,1,0:T(8,128)(2,1)S(1)} all-to-all(bf16[4,144,256]{2,1,0:T(8,128)(2,1)S(1)} %near_sum.1), channel_id=1, replica_groups=mesh['xl'=2,'z'=8,'yh'=4,'yl'=2,'xh'=2,'c'=2] {'yh'}, dimensions={0} | all-to-all | bytes 589824 | tf_op jit(solution)/shard_map/all_to_all | solution.py:200
  85.5 0.0 copy-done.5
  85.5 0.2 delta.1
  85.7 17.4 %all_to_all.44.pieces_ref = bf16[16,16,256]{2,1,0:T(8,128)(2,1)S(1)} all-to-all(bf16[16,16,256]{2,1,0:T(8,128)(2,1)S(1)} %get-tuple-element.8), channel_id=1, replica_groups=mesh['xl'=2,'z'=8,'yh'=4,'yl'=2,'xh'=2,'c'=2] {'xl','z'}, dimensions={0} | all-to-all | bytes 262144 | tf_op jit(solution)/shard_map/all_to_all | solution.py:205
  103.1 0.6 mates.1
  103.6 10.5 %all_to_all.45.pieces_ref = bf16[16,16,256]{2,1,0:T(8,128)(2,1)S(1)} all-to-all(bf16[16,16,256]{2,1,0:T(8,128)(2,1)S(1)} %mates.1), channel_id=1, replica_groups=mesh['xl'=2,'z'=8,'yh'=4,'yl'=2,'xh'=2,'c'=2] {'xl','z'}, dimensions={0} | all-to-all | bytes 262144 | tf_op jit(solution)/shard_map/all_to_all | solution.py:207
  114.1 0.0 copy-done.4
  114.1 0.8 update.1
  114.9 13.3 %all_to_all.46 = bf16[4,144,256]{2,1,0:T(8,128)(2,1)S(1)} all-to-all(bf16[4,144,256]{2,1,0:T(8,128)(2,1)S(1)} %get-tuple-element.12), channel_id=1, replica_groups=mesh['xl'=2,'z'=8,'yh'=4,'yl'=2,'xh'=2,'c'=2] {'yh'}, dimensions={0} | all-to-all | bytes 589824 | tf_op jit(solution)/shard_map/all_to_all | solution.py:170
  128.2 0.1 broadcast_in_dim.24
  128.2 0.0 copy-start.3
  128.3 19.4 %all_to_all.47.mine_ref = bf16[4,4,144,256]{3,2,1,0:T(8,128)(2,1)S(1)} all-to-all(bf16[4,4,144,256]{3,2,1,0:T(8,128)(2,1)S(1)} %broadcast_in_dim.24), channel_id=1, replica_groups={{0,2,4,6},{8,10,12,14},{16,18,20,22},{24,26,28,30},{5,7,9,11},{13,15,17..., dimensions={0} | all-to-all | bytes 2359296 | tf_op jit(solution)/shard_map/all_to_all | solution.py:166
  147.7 4.1 %collective-permute-start.2 = (bf16[4,4,144,256]{3,2,1,0:T(8,128)(2,1)S(1)}, bf16[4,4,144,256]{3,2,1,0:T(8,128)(2,1)S(1)}, u32[]{:S(2)}, u32[]{:S(2)}) collective-permute-start(bf16[4,4,144,256]{3,2,1,0:T(8,128)(2,1)S(1)} %all_to_all.47.mine_ref), channel_id=1, source_target_pairs={{0,1},{1,0},{2,3},{3,2},{4,5},{5,4},{6,7},{7,6},{8,9},{9,8},{10,11... | collective-permute-start | bytes 3538952 | tf_op jit(solution)/shard_map/ppermute | solution.py:215
  151.7 2.5 %collective-permute-done.2.other_ref = bf16[4,4,144,256]{3,2,1,0:T(8,128)(2,1)S(1)} collective-permute-done((bf16[4,4,144,256]{3,2,1,0:T(8,128)(2,1)S(1)}, bf16[4,4,144,256]{3,2,1,0:T(8,128)(2,1)S(1)}, u32[]{:S(2)}, u32[]{:S(2)}) %collective-permute-start.2) | collective-permute-done | bytes 1179680 | tf_op jit(solution)/shard_map/ppermute | solution.py:215
  154.2 0.0 copy-done.3
  154.2 1.3 rollout.1
  (10 shorter events, 0.0 us)
Async XLA Ops:
  0.6 44.0 %collective-permute-start = (bf16[256,4608]{1,0:T(8,128)(2,1)}, bf16[256,4608]{1,0:T(8,128)(2,1)S(1)}, u32[]{:S(2)}, u32[]{:S(2)}) collective-permute-start(bf16[256,4608]{1,0:T(8,128)(2,1)} %bitcast.11), channel_id=1, source_target_pairs={{0,1},{1,0},{2,3},{3,2},{4,5},{5,4},{6,7},{7,6},{8,9},{9,8},{10,11... | collective-permute-start | bytes 7077896 | tf_op jit(solution)/shard_map/ppermute | solution.py:183
  9.4 0.9 copy-start.1
  23.5 21.1 %copy-start.7 = (bf16[1,256,256]{2,1,0:T(8,128)(2,1)S(1)}, bf16[1,256,256]{2,1,0:T(8,128)(2,1)}, u32[]{:S(2)}) copy-start(bf16[1,256,256]{2,1,0:T(8,128)(2,1)} %param.13) | copy-start | bytes 393220
  23.6 21.0 %copy-start = (bf16[1,256,4608]{2,1,0:T(8,128)(2,1)S(1)}, bf16[1,256,4608]{2,1,0:T(8,128)(2,1)}, u32[]{:S(2)}) copy-start(bf16[1,256,4608]{2,1,0:T(8,128)(2,1)} %param.12) | copy-start | bytes 7077892
  46.2 4.5 %collective-permute-start.1 = (f32[2,256,256]{2,1,0:T(8,128)S(1)}, f32[2,256,256]{2,1,0:T(8,128)S(1)}, u32[]{:S(2)}, u32[]{:S(2)}) collective-permute-start(f32[2,256,256]{2,1,0:T(8,128)S(1)} %pred_.1.here_ref), channel_id=1, source_target_pairs={{0,1},{1,0},{2,3},{3,2},{4,5},{5,4},{6,7},{7,6},{8,9},{9,8},{10,11... | collective-permute-start | bytes 1572872 | tf_op jit(solution)/shard_map/ppermute | solution.py:189
  72.5 13.0 %copy-start.2 = (f32[1,144,256]{2,1,0:T(8,128)S(1)}, f32[1,144,256]{2,1,0:T(8,128)}, u32[]{:S(2)}) copy-start(f32[1,144,256]{2,1,0:T(8,128)} %param.8) | copy-start | bytes 442372
  72.5 13.0 %copy-start.5 = (f32[1,144,256]{2,1,0:T(8,128)S(1)}, f32[1,144,256]{2,1,0:T(8,128)}, u32[]{:S(2)}) copy-start(f32[1,144,256]{2,1,0:T(8,128)} %param.10) | copy-start | bytes 442372
  72.5 13.0 %copy-start.6 = (f32[1,144,256]{2,1,0:T(8,128)S(1)}, f32[1,144,256]{2,1,0:T(8,128)}, u32[]{:S(2)}) copy-start(f32[1,144,256]{2,1,0:T(8,128)} %param.11) | copy-start | bytes 442372
  72.5 30.5 %copy-start.8 = (s32[16,1]{0,1:T(1,128)S(1)}, s32[16,1]{0,1:T(1,128)}, u32[]{:S(2)}) copy-start(s32[16,1]{0,1:T(1,128)} %param.15) | copy-start | bytes 196
  72.7 41.5 %copy-start.4 = (f32[1,144,256]{2,1,0:T(8,128)S(1)}, f32[1,144,256]{2,1,0:T(8,128)}, u32[]{:S(2)}) copy-start(f32[1,144,256]{2,1,0:T(8,128)} %param.9) | copy-start | bytes 442372
  128.2 25.9 %copy-start.3 = (bf16[1,128,4608]{2,1,0:T(8,128)(2,1)S(1)}, bf16[1,128,4608]{2,1,0:T(8,128)(2,1)}, u32[]{:S(2)}) copy-start(bf16[1,128,4608]{2,1,0:T(8,128)(2,1)} %param.14) | copy-start | bytes 3538948
  147.7 6.5 %collective-permute-start.2 = (bf16[4,4,144,256]{3,2,1,0:T(8,128)(2,1)S(1)}, bf16[4,4,144,256]{3,2,1,0:T(8,128)(2,1)S(1)}, u32[]{:S(2)}, u32[]{:S(2)}) collective-permute-start(bf16[4,4,144,256]{3,2,1,0:T(8,128)(2,1)S(1)} %all_to_all.47.mine_ref), channel_id=1, source_target_pairs={{0,1},{1,0},{2,3},{3,2},{4,5},{5,4},{6,7},{7,6},{8,9},{9,8},{10,11... | collective-permute-start | bytes 3538952 | tf_op jit(solution)/shard_map/ppermute | solution.py:215

commit v4 on v2

--- a/solution.py
+++ b/solution.py
@@ -120,24 +120,32 @@
         send_ref[j] = weight_ref[...].astype(bf16)
 
 
-def rollout_kernel(states_ref, mine_ref, other_ref, out_ref, full_ref):
+def place_kernel(mine_ref, full_ref):
     core = lax.axis_index("c")
     rows = mine_ref.shape[2]
     for far in range(NFAR):
         for near in range(NNEAR):
             full_ref[block_rows(far, near, core, rows), :] = mine_ref[near, far]
-            full_ref[block_rows(far, near, 1 - core, rows), :] = other_ref[near, far]
-    out = jnp.dot(states_ref[...], full_ref[...], preferred_element_type=f32) * scale
+
+
+def rollout_kernel(states_ref, other_ref, full_ref, out_ref, whole_ref):
+    core = lax.axis_index("c")
+    rows = other_ref.shape[2]
+    for far in range(NFAR):
+        for near in range(NNEAR):
+            whole_ref[block_rows(far, near, 1 - core, rows), :] = other_ref[near, far]
+    out = jnp.dot(states_ref[...], whole_ref[...], preferred_element_type=f32) * scale
     out_ref[...] = out.astype(bf16)
 
 
-def call(kernel, out, ins, scratch=(), name=None, mib=6):
+def call(kernel, out, ins, scratch=(), name=None, mib=6, alias=None):
     run = pl.pallas_call(
         kernel,
         out_shape=out,
         in_specs=[SMEM if space == "s" else VMEM for space in ins],
         out_specs=jax.tree.map(lambda _: VMEM, out),
         scratch_shapes=scratch,
+        input_output_aliases=alias or {},
         compiler_params=pltpu.CompilerParams(vmem_limit_bytes=mib << 20),
         name=name,
     )
@@ -193,20 +201,21 @@
     pieces = lax.all_to_all(pieces, GRP, 0, 0)
     new_weight, new_momentum, send = call(
         update_kernel,
-        (S((rows, width), f32), S((rows, width), f32), V((NFAR, rows, width), bf16)),
+        (V((rows, width), f32), V((rows, width), f32), V((NFAR, rows, width), bf16)),
         "vvvv",
         name="update",
     )(pieces, delta, weight, momentum)
     mine = gather_rows(send)
     other = lax.ppermute(mine, "c", SWAP)
-    rollout = call(
+    full = call(place_kernel, V((depth, width), bf16), "v", name="place")(mine)
+    rollout, _ = call(
         rollout_kernel,
-        S((states.shape[0], width), bf16),
+        (S((states.shape[0], width), bf16), V((depth, width), bf16)),
         "vvv",
-        [pltpu.VMEM((depth, width), bf16)],
-        "rollout",
-        12,
-    )(states, mine, other)
+        name="rollout",
+        mib=8,
+        alias={2: 1},
+    )(states, other, full)
     return new_weight[None], new_momentum[None], rollout[None]
 
 

time: 154 us -> 153 us (level)
    pallas_call x8 -> x9, Pallas kernels: 6.65 us -> 5.87 us  [apply(): return run(*held)]
  transfers between devices with their start and end apart: 3 -> 3, of which waited for: 2 -> 2; matrix products, arithmetic and copies ran while one was open for 0% -> 1% of each run, Pallas kernels for 0% -> 0%
where the time goes in v4:
time: 153 us; the launch traced here: 152 us
  blocking collectives  116 us (76%)
  starting transfers between devices  24.1 us (16%)
  Pallas kernels  5.87 us (4%)
  local copies, waits for them, and re-layouts  2.56 us (2%)
  waiting for transfers between devices  2.55 us (2%)
    all_to_all x2, blocking collectives, gather_rows(): lax.all_to_all(jnp.broadcast_to(far[None], (NNEAR,) + far.shape), NEAR, 0...  30.4 us
    all_to_all x2, blocking collectives, shards(): pieces = lax.all_to_all(pieces, GRP, 0, 0)  27.6 us
    all_to_all x2, blocking collectives, gather_rows(): far = lax.all_to_all(send, FAR, 0, 0)  27.1 us
    all_to_all x1, blocking collectives, shards(): near = lax.all_to_all(grads, NEAR, 0, 0)  18.9 us
    all_to_all x1, blocking collectives, shards(): far = lax.all_to_all(near, FAR, 0, 0)  12.5 us
    ppermute x1, starting transfers between devices, shards(): other = lax.ppermute(mine, 'c', SWAP)  9.07 us
    ppermute x1, starting transfers between devices, shards(): inputs_other = lax.ppermute(inputs, 'c', SWAP)  8.75 us
    ppermute x1, starting transfers between devices, shards(): there = lax.ppermute(here, 'c', SWAP)  6.29 us
  transfers between devices with their start and end apart: 3, of which 2 were waited for; matrix products, arithmetic and copies ran while one was open for 1% of the time, Pallas kernels for 0%

profile of v4, /device:TPU:1, one launch (start us, length us, event | category | flops | bytes accessed | tf_op | source)
XLA Modules:
  0.0 152.3 jit_solution(11678803003155779756)
XLA Ops:
  0.6 8.7 %collective-permute-start = (bf16[256,4608]{1,0:T(8,128)(2,1)}, bf16[256,4608]{1,0:T(8,128)(2,1)S(1)}, u32[]{:S(2)}, u32[]{:S(2)}) collective-permute-start(bf16[256,4608]{1,0:T(8,128)(2,1)} %bitcast.13), channel_id=1, source_target_pairs={{0,1},{1,0},{2,3},{3,2},{4,5},{5,4},{6,7},{7,6},{8,9},{9,8},{10,11... | collective-permute-start | bytes 7077896 | tf_op jit(solution)/shard_map/ppermute | solution.py:177
  9.4 0.0 copy-start.1
  9.4 0.9 copy-done.1
  10.3 13.2 %all_to_all.40 = bf16[4,144,256]{2,1,0:T(8,128)(2,1)S(1)} all-to-all(bf16[4,144,256]{2,1,0:T(8,128)(2,1)S(1)} %cast.1), channel_id=1, replica_groups=mesh['xl'=2,'z'=8,'yh'=4,'yl'=2,'xh'=2,'c'=2] {'yh'}, dimensions={0} | all-to-all | bytes 589824 | tf_op jit(solution)/shard_map/all_to_all | solution.py:164
  23.5 0.1 broadcast_in_dim.10
  23.6 0.0 copy-start
  23.6 16.2 %all_to_all.41.weight_ref = bf16[4,4,144,256]{3,2,1,0:T(8,128)(2,1)S(1)} all-to-all(bf16[4,4,144,256]{3,2,1,0:T(8,128)(2,1)S(1)} %broadcast_in_dim.10), channel_id=1, replica_groups=mesh['xl'=2,'z'=8,'yh'=4,'yl'=2,'xh'=2,'c'=2] {'yl','xh'}, dimensions={0} | all-to-all | bytes 2359296 | tf_op jit(solution)/shard_map/all_to_all | solution.py:165
  39.8 0.0 collective-permute-done.other_ref
  39.8 0.0 copy-done
  39.8 1.4 pred_.1.here_ref
  41.2 6.3 %collective-permute-start.1 = (f32[2,256,256]{2,1,0:T(8,128)S(1)}, f32[2,256,256]{2,1,0:T(8,128)S(1)}, u32[]{:S(2)}, u32[]{:S(2)}) collective-permute-start(f32[2,256,256]{2,1,0:T(8,128)S(1)} %pred_.1.here_ref), channel_id=1, source_target_pairs={{0,1},{1,0},{2,3},{3,2},{4,5},{5,4},{6,7},{7,6},{8,9},{9,8},{10,11... | collective-permute-start | bytes 1572872 | tf_op jit(solution)/shard_map/ppermute | solution.py:183
  47.5 1.5 collective-permute-done.1.there_ref
  49.1 2.1 %grad.1 = bf16[4,4,144,256]{3,2,1,0:T(8,128)(2,1)S(1)} custom-call(bf16[256,4608]{1,0:T(8,128)(2,1)S(1)} %bitcast.15, bf16[256,4608]{1,0:T(8,128)(2,1)S(1)} %collective-permute-done.other_ref, f32[2,256,256]{2,1,0:T(8,128)S(1)} %pred_.1.here_ref, f32[2,256,256]{2,1,0:T(8,128)S(1)} %collective-permute-done.1.there_ref), custom_call_target="tpu_custom_call" | custom-call | tf_op jit(solution)/shard_map/grad/pallas_call | solution.py:158
  51.2 18.9 %all_to_all.42.parts_ref = bf16[4,4,144,256]{3,2,1,0:T(8,128)(2,1)S(1)} all-to-all(bf16[4,4,144,256]{3,2,1,0:T(8,128)(2,1)S(1)} %grad.1), channel_id=1, replica_groups=mesh['xl'=2,'z'=8,'yh'=4,'yl'=2,'xh'=2,'c'=2] {'yl','xh'}, dimensions={0} | all-to-all | bytes 2359296 | tf_op jit(solution)/shard_map/all_to_all | solution.py:192
  70.1 0.1 near_sum.1
  70.2 0.0 copy-start.4
  70.2 12.5 %all_to_all.43.parts_ref = bf16[4,144,256]{2,1,0:T(8,128)(2,1)S(1)} all-to-all(bf16[4,144,256]{2,1,0:T(8,128)(2,1)S(1)} %near_sum.1), channel_id=1, replica_groups=mesh['xl'=2,'z'=8,'yh'=4,'yl'=2,'xh'=2,'c'=2] {'yh'}, dimensions={0} | all-to-all | bytes 589824 | tf_op jit(solution)/shard_map/all_to_all | solution.py:194
  82.8 0.2 delta.1
  82.9 17.4 %all_to_all.44.pieces_ref = bf16[16,16,256]{2,1,0:T(8,128)(2,1)S(1)} all-to-all(bf16[16,16,256]{2,1,0:T(8,128)(2,1)S(1)} %get-tuple-element.9), channel_id=1, replica_groups=mesh['xl'=2,'z'=8,'yh'=4,'yl'=2,'xh'=2,'c'=2] {'xl','z'}, dimensions={0} | all-to-all | bytes 262144 | tf_op jit(solution)/shard_map/all_to_all | solution.py:199
  100.3 0.6 mates.1
  100.9 10.2 %all_to_all.45.pieces_ref = bf16[16,16,256]{2,1,0:T(8,128)(2,1)S(1)} all-to-all(bf16[16,16,256]{2,1,0:T(8,128)(2,1)S(1)} %mates.1), channel_id=1, replica_groups=mesh['xl'=2,'z'=8,'yh'=4,'yl'=2,'xh'=2,'c'=2] {'xl','z'}, dimensions={0} | all-to-all | bytes 262144 | tf_op jit(solution)/shard_map/all_to_all | solution.py:201
  111.1 0.1 update.1
  111.2 13.9 %all_to_all.46 = bf16[4,144,256]{2,1,0:T(8,128)(2,1)S(1)} all-to-all(bf16[4,144,256]{2,1,0:T(8,128)(2,1)S(1)} %get-tuple-element.13), channel_id=1, replica_groups=mesh['xl'=2,'z'=8,'yh'=4,'yl'=2,'xh'=2,'c'=2] {'yh'}, dimensions={0} | all-to-all | bytes 589824 | tf_op jit(solution)/shard_map/all_to_all | solution.py:164
  125.1 0.1 broadcast_in_dim.24
  125.1 14.2 %all_to_all.47.mine_ref = bf16[4,4,144,256]{3,2,1,0:T(8,128)(2,1)S(1)} all-to-all(bf16[4,4,144,256]{3,2,1,0:T(8,128)(2,1)S(1)} %broadcast_in_dim.24), channel_id=1, replica_groups=mesh['xl'=2,'z'=8,'yh'=4,'yl'=2,'xh'=2,'c'=2] {'yl','xh'}, dimensions={0} | all-to-all | bytes 2359296 | tf_op jit(solution)/shard_map/all_to_all | solution.py:165
  139.3 9.1 %collective-permute-start.2 = (bf16[4,4,144,256]{3,2,1,0:T(8,128)(2,1)S(1)}, bf16[4,4,144,256]{3,2,1,0:T(8,128)(2,1)S(1)}, u32[]{:S(2)}, u32[]{:S(2)}) collective-permute-start(bf16[4,4,144,256]{3,2,1,0:T(8,128)(2,1)S(1)} %all_to_all.47.mine_ref), channel_id=1, source_target_pairs={{0,1},{1,0},{2,3},{3,2},{4,5},{5,4},{6,7},{7,6},{8,9},{9,8},{10,11... | collective-permute-start | bytes 3538952 | tf_op jit(solution)/shard_map/ppermute | solution.py:209
  148.4 0.7 copy.13
  149.1 0.7 copy.14
  149.8 0.1 place.1.full_ref
  149.8 1.0 collective-permute-done.2.other_ref
  150.9 0.1 copy-done.3
  151.0 1.3 rollout.1
  (13 shorter events, 0.0 us)
Async XLA Ops:
  0.6 39.2 %collective-permute-start = (bf16[256,4608]{1,0:T(8,128)(2,1)}, bf16[256,4608]{1,0:T(8,128)(2,1)S(1)}, u32[]{:S(2)}, u32[]{:S(2)}) collective-permute-start(bf16[256,4608]{1,0:T(8,128)(2,1)} %bitcast.13), channel_id=1, source_target_pairs={{0,1},{1,0},{2,3},{3,2},{4,5},{5,4},{6,7},{7,6},{8,9},{9,8},{10,11... | collective-permute-start | bytes 7077896 | tf_op jit(solution)/shard_map/ppermute | solution.py:177
  9.4 0.9 copy-start.1
  23.5 16.3 %copy-start.7 = (bf16[1,256,256]{2,1,0:T(8,128)(2,1)S(1)}, bf16[1,256,256]{2,1,0:T(8,128)(2,1)}, u32[]{:S(2)}) copy-start(bf16[1,256,256]{2,1,0:T(8,128)(2,1)} %param.13) | copy-start | bytes 393220
  23.6 16.2 %copy-start = (bf16[1,256,4608]{2,1,0:T(8,128)(2,1)S(1)}, bf16[1,256,4608]{2,1,0:T(8,128)(2,1)}, u32[]{:S(2)}) copy-start(bf16[1,256,4608]{2,1,0:T(8,128)(2,1)} %param.12) | copy-start | bytes 7077892
  41.2 7.8 %collective-permute-start.1 = (f32[2,256,256]{2,1,0:T(8,128)S(1)}, f32[2,256,256]{2,1,0:T(8,128)S(1)}, u32[]{:S(2)}, u32[]{:S(2)}) collective-permute-start(f32[2,256,256]{2,1,0:T(8,128)S(1)} %pred_.1.here_ref), channel_id=1, source_target_pairs={{0,1},{1,0},{2,3},{3,2},{4,5},{5,4},{6,7},{7,6},{8,9},{9,8},{10,11... | collective-permute-start | bytes 1572872 | tf_op jit(solution)/shard_map/ppermute | solution.py:183
  70.1 12.7 %copy-start.2 = (f32[1,144,256]{2,1,0:T(8,128)S(1)}, f32[1,144,256]{2,1,0:T(8,128)}, u32[]{:S(2)}) copy-start(f32[1,144,256]{2,1,0:T(8,128)} %param.8) | copy-start | bytes 442372
  70.1 12.7 %copy-start.5 = (f32[1,144,256]{2,1,0:T(8,128)S(1)}, f32[1,144,256]{2,1,0:T(8,128)}, u32[]{:S(2)}) copy-start(f32[1,144,256]{2,1,0:T(8,128)} %param.10) | copy-start | bytes 442372
  70.1 12.7 %copy-start.6 = (f32[1,144,256]{2,1,0:T(8,128)S(1)}, f32[1,144,256]{2,1,0:T(8,128)}, u32[]{:S(2)}) copy-start(f32[1,144,256]{2,1,0:T(8,128)} %param.11) | copy-start | bytes 442372
  70.1 30.3 %copy-start.8 = (s32[16,1]{0,1:T(1,128)S(1)}, s32[16,1]{0,1:T(1,128)}, u32[]{:S(2)}) copy-start(s32[16,1]{0,1:T(1,128)} %param.15) | copy-start | bytes 196
  70.2 40.9 %copy-start.4 = (f32[1,144,256]{2,1,0:T(8,128)S(1)}, f32[1,144,256]{2,1,0:T(8,128)}, u32[]{:S(2)}) copy-start(f32[1,144,256]{2,1,0:T(8,128)} %param.9) | copy-start | bytes 442372
  139.3 11.5 %collective-permute-start.2 = (bf16[4,4,144,256]{3,2,1,0:T(8,128)(2,1)S(1)}, bf16[4,4,144,256]{3,2,1,0:T(8,128)(2,1)S(1)}, u32[]{:S(2)}, u32[]{:S(2)}) collective-permute-start(bf16[4,4,144,256]{3,2,1,0:T(8,128)(2,1)S(1)} %all_to_all.47.mine_ref), channel_id=1, source_target_pairs={{0,1},{1,0},{2,3},{3,2},{4,5},{5,4},{6,7},{7,6},{8,9},{9,8},{10,11... | collective-permute-start | bytes 3538952 | tf_op jit(solution)/shard_map/ppermute | solution.py:209
  149.8 1.3 copy-start.3

commit v5 on v4

--- a/solution.py
+++ b/solution.py
@@ -43,7 +43,7 @@
     return pl.ds(pl.multiple_of(start, 16), rows)
 
 
-def pred_kernel(mine_ref, other_ref, weight_ref, target_ref, out_ref, full_ref):
+def pred_kernel(mine_ref, other_ref, weight_ref, target_ref, out_ref, send_ref, full_ref):
     core = lax.axis_index("c")
     rows = weight_ref.shape[2]
     for far in range(NFAR):
@@ -51,16 +51,20 @@
             full_ref[block_rows(far, near, core, rows), :] = weight_ref[near, far]
             full_ref[block_rows(far, near, 1 - core, rows), :] = jnp.zeros_like(weight_ref[near, far])
     mine = jnp.dot(mine_ref[...], full_ref[...], preferred_element_type=f32)
-    out_ref[0] = mine * scale - target_ref[...].astype(f32)
+    mine = mine * scale - target_ref[...].astype(f32)
+    out_ref[0] = mine
+    send_ref[0] = mine.astype(bf16)
     other = jnp.dot(other_ref[...], full_ref[...], preferred_element_type=f32)
-    out_ref[1] = other * scale
+    other = other * scale
+    out_ref[1] = other
+    send_ref[1] = other.astype(bf16)
 
 
 def grad_kernel(tokens, mine_ref, other_ref, here_ref, there_ref, out_ref, part_ref):
     core = lax.axis_index("c")
     rows = out_ref.shape[2]
-    resid_mine = ((here_ref[0] + there_ref[1]) / tokens).astype(bf16)
-    resid_other = ((here_ref[1] + there_ref[0]) / tokens).astype(bf16)
+    resid_mine = ((here_ref[0] + there_ref[1].astype(f32)) / tokens).astype(bf16)
+    resid_other = ((here_ref[1] + there_ref[0].astype(f32)) / tokens).astype(bf16)
     dims = (((0,), (0,)), ((), ()))
     span = 2 * NNEAR * rows
     for far in range(NFAR):
@@ -177,10 +181,11 @@
     inputs_other = lax.ppermute(inputs, "c", SWAP)
     send = call(cast_kernel, V((NFAR, rows, width), bf16), "h", name="cast")(weight)
     parts = gather_rows(send)
-    here = call(
-        pred_kernel, V((2, count, width), f32), "vvvv", [pltpu.VMEM((depth, width), bf16)], "pred", 16
+    shape = (2, count, width)
+    here, sent = call(
+        pred_kernel, (V(shape, f32), V(shape, bf16)), "vvvv", [pltpu.VMEM((depth, width), bf16)], "pred", 16
     )(inputs, inputs_other, parts, targets)
-    there = lax.ppermute(here, "c", SWAP)
+    there = lax.ppermute(sent, "c", SWAP)
     grads = call(
         functools.partial(grad_kernel, tokens_all),
         V((NNEAR, NFAR, rows, width), bf16),

time: 153 us -> 152 us (level)
  no operation moved by 1% of the time
where the time goes in v5:
time: 152 us
  blocking collectives  116 us (76%)
  starting transfers between devices  24.1 us (16%)
  Pallas kernels  5.87 us (4%)
  local copies, waits for them, and re-layouts  2.56 us (2%)
  waiting for transfers between devices  2.18 us (1%)
    all_to_all x2, blocking collectives, gather_rows(): lax.all_to_all(jnp.broadcast_to(far[None], (NNEAR,) + far.shape), NEAR, 0...  30.4 us
    all_to_all x2, blocking collectives, shards(): pieces = lax.all_to_all(pieces, GRP, 0, 0)  27.6 us
    all_to_all x2, blocking collectives, gather_rows(): far = lax.all_to_all(send, FAR, 0, 0)  27.1 us
    all_to_all x1, blocking collectives, shards(): near = lax.all_to_all(grads, NEAR, 0, 0)  18.9 us
    all_to_all x1, blocking collectives, shards(): far = lax.all_to_all(near, FAR, 0, 0)  12.5 us
    ppermute x1, starting transfers between devices, shards(): other = lax.ppermute(mine, 'c', SWAP)  9.07 us
    ppermute x1, starting transfers between devices, shards(): inputs_other = lax.ppermute(inputs, 'c', SWAP)  8.75 us
    ppermute x1, starting transfers between devices, shards(): there = lax.ppermute(sent, 'c', SWAP)  6.29 us
  transfers between devices with their start and end apart: 3, of which 2 were waited for; matrix products, arithmetic and copies ran while one was open for 1% of the time, Pallas kernels for 0%

profile of v5, /device:TPU:1, one launch (start us, length us, event | category | flops | bytes accessed | tf_op | source)
XLA Modules:
  0.0 152.0 jit_solution(11937980481536399497)
XLA Ops:
  0.6 8.7 %collective-permute-start = (bf16[256,4608]{1,0:T(8,128)(2,1)}, bf16[256,4608]{1,0:T(8,128)(2,1)S(1)}, u32[]{:S(2)}, u32[]{:S(2)}) collective-permute-start(bf16[256,4608]{1,0:T(8,128)(2,1)} %bitcast.13), channel_id=1, source_target_pairs={{0,1},{1,0},{2,3},{3,2},{4,5},{5,4},{6,7},{7,6},{8,9},{9,8},{10,11... | collective-permute-start | bytes 7077896 | tf_op jit(solution)/shard_map/ppermute | solution.py:181
  9.4 0.0 copy-start.1
  9.4 0.9 copy-done.1
  10.3 13.2 %all_to_all.40 = bf16[4,144,256]{2,1,0:T(8,128)(2,1)S(1)} all-to-all(bf16[4,144,256]{2,1,0:T(8,128)(2,1)S(1)} %cast.1), channel_id=1, replica_groups=mesh['xl'=2,'z'=8,'yh'=4,'yl'=2,'xh'=2,'c'=2] {'yh'}, dimensions={0} | all-to-all | bytes 589824 | tf_op jit(solution)/shard_map/all_to_all | solution.py:168
  23.5 0.1 broadcast_in_dim.10
  23.6 0.0 copy-start
  23.6 16.2 %all_to_all.41.weight_ref = bf16[4,4,144,256]{3,2,1,0:T(8,128)(2,1)S(1)} all-to-all(bf16[4,4,144,256]{3,2,1,0:T(8,128)(2,1)S(1)} %broadcast_in_dim.10), channel_id=1, replica_groups=mesh['xl'=2,'z'=8,'yh'=4,'yl'=2,'xh'=2,'c'=2] {'yl','xh'}, dimensions={0} | all-to-all | bytes 2359296 | tf_op jit(solution)/shard_map/all_to_all | solution.py:169
  39.8 0.0 collective-permute-done.other_ref
  39.8 0.0 copy-done
  39.8 1.4 pred_.1
  41.2 6.3 %collective-permute-start.1 = (bf16[2,256,256]{2,1,0:T(8,128)(2,1)S(1)}, bf16[2,256,256]{2,1,0:T(8,128)(2,1)S(1)}, u32[]{:S(2)}, u32[]{:S(2)}) collective-permute-start(bf16[2,256,256]{2,1,0:T(8,128)(2,1)S(1)} %get-tuple-element.12), channel_id=1, source_target_pairs={{0,1},{1,0},{2,3},{3,2},{4,5},{5,4},{6,7},{7,6},{8,9},{9,8},{10,11... | collective-permute-start | bytes 786440 | tf_op jit(solution)/shard_map/ppermute | solution.py:188
  47.5 1.1 collective-permute-done.1.there_ref
  48.7 2.1 %grad.1 = bf16[4,4,144,256]{3,2,1,0:T(8,128)(2,1)S(1)} custom-call(bf16[256,4608]{1,0:T(8,128)(2,1)S(1)} %bitcast.15, bf16[256,4608]{1,0:T(8,128)(2,1)S(1)} %collective-permute-done.other_ref, f32[2,256,256]{2,1,0:T(8,128)S(1)} %get-tuple-element.11.here_ref, bf16[2,256,256]{2,1,0:T(8,128)(2,1)S(1)} %collective-permute-done.1.there_ref), custom_call_target="tpu_custom_call" | custom-call | tf_op jit(solution)/shard_map/grad/pallas_call | solution.py:162
  50.8 18.9 %all_to_all.42.parts_ref = bf16[4,4,144,256]{3,2,1,0:T(8,128)(2,1)S(1)} all-to-all(bf16[4,4,144,256]{3,2,1,0:T(8,128)(2,1)S(1)} %grad.1), channel_id=1, replica_groups=mesh['xl'=2,'z'=8,'yh'=4,'yl'=2,'xh'=2,'c'=2] {'yl','xh'}, dimensions={0} | all-to-all | bytes 2359296 | tf_op jit(solution)/shard_map/all_to_all | solution.py:197
  69.7 0.1 near_sum.1
  69.9 0.0 copy-start.4
  69.9 12.5 %all_to_all.43.parts_ref = bf16[4,144,256]{2,1,0:T(8,128)(2,1)S(1)} all-to-all(bf16[4,144,256]{2,1,0:T(8,128)(2,1)S(1)} %near_sum.1), channel_id=1, replica_groups=mesh['xl'=2,'z'=8,'yh'=4,'yl'=2,'xh'=2,'c'=2] {'yh'}, dimensions={0} | all-to-all | bytes 589824 | tf_op jit(solution)/shard_map/all_to_all | solution.py:199
  82.4 0.2 delta.1
  82.6 17.4 %all_to_all.44.pieces_ref = bf16[16,16,256]{2,1,0:T(8,128)(2,1)S(1)} all-to-all(bf16[16,16,256]{2,1,0:T(8,128)(2,1)S(1)} %get-tuple-element.13), channel_id=1, replica_groups=mesh['xl'=2,'z'=8,'yh'=4,'yl'=2,'xh'=2,'c'=2] {'xl','z'}, dimensions={0} | all-to-all | bytes 262144 | tf_op jit(solution)/shard_map/all_to_all | solution.py:204
  100.0 0.6 mates.1
  100.5 10.2 %all_to_all.45.pieces_ref = bf16[16,16,256]{2,1,0:T(8,128)(2,1)S(1)} all-to-all(bf16[16,16,256]{2,1,0:T(8,128)(2,1)S(1)} %mates.1), channel_id=1, replica_groups=mesh['xl'=2,'z'=8,'yh'=4,'yl'=2,'xh'=2,'c'=2] {'xl','z'}, dimensions={0} | all-to-all | bytes 262144 | tf_op jit(solution)/shard_map/all_to_all | solution.py:206
  110.7 0.1 update.1
  110.8 13.9 %all_to_all.46 = bf16[4,144,256]{2,1,0:T(8,128)(2,1)S(1)} all-to-all(bf16[4,144,256]{2,1,0:T(8,128)(2,1)S(1)} %get-tuple-element.17), channel_id=1, replica_groups=mesh['xl'=2,'z'=8,'yh'=4,'yl'=2,'xh'=2,'c'=2] {'yh'}, dimensions={0} | all-to-all | bytes 589824 | tf_op jit(solution)/shard_map/all_to_all | solution.py:168
  124.7 0.1 broadcast_in_dim.24
  124.8 14.2 %all_to_all.47.mine_ref = bf16[4,4,144,256]{3,2,1,0:T(8,128)(2,1)S(1)} all-to-all(bf16[4,4,144,256]{3,2,1,0:T(8,128)(2,1)S(1)} %broadcast_in_dim.24), channel_id=1, replica_groups=mesh['xl'=2,'z'=8,'yh'=4,'yl'=2,'xh'=2,'c'=2] {'yl','xh'}, dimensions={0} | all-to-all | bytes 2359296 | tf_op jit(solution)/shard_map/all_to_all | solution.py:169
  139.0 9.1 %collective-permute-start.2 = (bf16[4,4,144,256]{3,2,1,0:T(8,128)(2,1)S(1)}, bf16[4,4,144,256]{3,2,1,0:T(8,128)(2,1)S(1)}, u32[]{:S(2)}, u32[]{:S(2)}) collective-permute-start(bf16[4,4,144,256]{3,2,1,0:T(8,128)(2,1)S(1)} %all_to_all.47.mine_ref), channel_id=1, source_target_pairs={{0,1},{1,0},{2,3},{3,2},{4,5},{5,4},{6,7},{7,6},{8,9},{9,8},{10,11... | collective-permute-start | bytes 3538952 | tf_op jit(solution)/shard_map/ppermute | solution.py:214
  148.1 0.7 copy.13
  148.7 0.7 copy.14
  149.4 0.1 place.1.full_ref
  149.5 1.0 collective-permute-done.2.other_ref
  150.5 0.1 copy-done.3
  150.7 1.3 rollout.1
  (13 shorter events, 0.0 us)
Async XLA Ops:
  0.6 39.2 %collective-permute-start = (bf16[256,4608]{1,0:T(8,128)(2,1)}, bf16[256,4608]{1,0:T(8,128)(2,1)S(1)}, u32[]{:S(2)}, u32[]{:S(2)}) collective-permute-start(bf16[256,4608]{1,0:T(8,128)(2,1)} %bitcast.13), channel_id=1, source_target_pairs={{0,1},{1,0},{2,3},{3,2},{4,5},{5,4},{6,7},{7,6},{8,9},{9,8},{10,11... | collective-permute-start | bytes 7077896 | tf_op jit(solution)/shard_map/ppermute | solution.py:181
  9.4 0.9 copy-start.1
  23.5 16.3 %copy-start.7 = (bf16[1,256,256]{2,1,0:T(8,128)(2,1)S(1)}, bf16[1,256,256]{2,1,0:T(8,128)(2,1)}, u32[]{:S(2)}) copy-start(bf16[1,256,256]{2,1,0:T(8,128)(2,1)} %param.13) | copy-start | bytes 393220
  23.6 16.2 %copy-start = (bf16[1,256,4608]{2,1,0:T(8,128)(2,1)S(1)}, bf16[1,256,4608]{2,1,0:T(8,128)(2,1)}, u32[]{:S(2)}) copy-start(bf16[1,256,4608]{2,1,0:T(8,128)(2,1)} %param.12) | copy-start | bytes 7077892
  41.2 7.4 %collective-permute-start.1 = (bf16[2,256,256]{2,1,0:T(8,128)(2,1)S(1)}, bf16[2,256,256]{2,1,0:T(8,128)(2,1)S(1)}, u32[]{:S(2)}, u32[]{:S(2)}) collective-permute-start(bf16[2,256,256]{2,1,0:T(8,128)(2,1)S(1)} %get-tuple-element.12), channel_id=1, source_target_pairs={{0,1},{1,0},{2,3},{3,2},{4,5},{5,4},{6,7},{7,6},{8,9},{9,8},{10,11... | collective-permute-start | bytes 786440 | tf_op jit(solution)/shard_map/ppermute | solution.py:188
  69.7 12.7 %copy-start.2 = (f32[1,144,256]{2,1,0:T(8,128)S(1)}, f32[1,144,256]{2,1,0:T(8,128)}, u32[]{:S(2)}) copy-start(f32[1,144,256]{2,1,0:T(8,128)} %param.8) | copy-start | bytes 442372
  69.7 12.7 %copy-start.5 = (f32[1,144,256]{2,1,0:T(8,128)S(1)}, f32[1,144,256]{2,1,0:T(8,128)}, u32[]{:S(2)}) copy-start(f32[1,144,256]{2,1,0:T(8,128)} %param.10) | copy-start | bytes 442372
  69.7 12.7 %copy-start.6 = (f32[1,144,256]{2,1,0:T(8,128)S(1)}, f32[1,144,256]{2,1,0:T(8,128)}, u32[]{:S(2)}) copy-start(f32[1,144,256]{2,1,0:T(8,128)} %param.11) | copy-start | bytes 442372
  69.7 30.2 %copy-start.8 = (s32[16,1]{0,1:T(1,128)S(1)}, s32[16,1]{0,1:T(1,128)}, u32[]{:S(2)}) copy-start(s32[16,1]{0,1:T(1,128)} %param.15) | copy-start | bytes 196
  69.9 40.9 %copy-start.4 = (f32[1,144,256]{2,1,0:T(8,128)S(1)}, f32[1,144,256]{2,1,0:T(8,128)}, u32[]{:S(2)}) copy-start(f32[1,144,256]{2,1,0:T(8,128)} %param.9) | copy-start | bytes 442372
  139.0 11.5 %collective-permute-start.2 = (bf16[4,4,144,256]{3,2,1,0:T(8,128)(2,1)S(1)}, bf16[4,4,144,256]{3,2,1,0:T(8,128)(2,1)S(1)}, u32[]{:S(2)}, u32[]{:S(2)}) collective-permute-start(bf16[4,4,144,256]{3,2,1,0:T(8,128)(2,1)S(1)} %all_to_all.47.mine_ref), channel_id=1, source_target_pairs={{0,1},{1,0},{2,3},{3,2},{4,5},{5,4},{6,7},{7,6},{8,9},{9,8},{10,11... | collective-permute-start | bytes 3538952 | tf_op jit(solution)/shard_map/ppermute | solution.py:214
  149.4 1.3 copy-start.3

commit v6 on v5

--- a/solution.py
+++ b/solution.py
@@ -69,11 +69,15 @@
     span = 2 * NNEAR * rows
     for far in range(NFAR):
         cols = pl.ds(far * span, span)
-        part_ref[far] = lax.dot_general(
-            mine_ref[:, cols], resid_mine, dims, preferred_element_type=f32
+        part_ref[far] = jnp.dot(
+            mine_ref[cols, :], resid_mine, preferred_element_type=f32
         ) + lax.dot_general(other_ref[:, cols], resid_other, dims, preferred_element_type=f32)
         for near in range(NNEAR):
             out_ref[near, far] = part_ref[far, block_rows(0, near, core, rows), :].astype(bf16)
+
+
+def turn_kernel(tokens_ref, out_ref):
+    out_ref[...] = tokens_ref[...].T
 
 
 def sum_kernel(parts_ref, out_ref):
@@ -186,6 +190,8 @@
         pred_kernel, (V(shape, f32), V(shape, bf16)), "vvvv", [pltpu.VMEM((depth, width), bf16)], "pred", 16
     )(inputs, inputs_other, parts, targets)
     there = lax.ppermute(sent, "c", SWAP)
+    held, here = lax.optimization_barrier((inputs, here))
+    turned = call(turn_kernel, V((depth, count), bf16), "v", name="turn", mib=8)(held)
     grads = call(
         functools.partial(grad_kernel, tokens_all),
         V((NNEAR, NFAR, rows, width), bf16),
@@ -193,7 +199,7 @@
         [pltpu.VMEM((NFAR, 2 * NNEAR * rows, width), f32)],
         "grad",
         20,
-    )(inputs, inputs_other, here, there)
+    )(turned, inputs_other, here, there)
     near = lax.all_to_all(grads, NEAR, 0, 0)
     near = call(sum_kernel, V((NFAR, rows, width), bf16), "v", name="near_sum")(near)
     far = lax.all_to_all(near, FAR, 0, 0)

time: 152 us -> 152 us (level)
    pallas_call x9 -> x10, Pallas kernels: 5.87 us -> 6.27 us  [apply(): return run(*held)]
  transfers between devices with their start and end apart: 3 -> 3, of which waited for: 2 -> 2; matrix products, arithmetic and copies ran while one was open for 1% -> 1% of each run, Pallas kernels for 0% -> 1%
where the time goes in v6:
time: 152 us
  blocking collectives  117 us (77%)
  starting transfers between devices  24.1 us (16%)
  Pallas kernels  6.27 us (4%)
  local copies, waits for them, and re-layouts  2.56 us (2%)
  waiting for transfers between devices  1.52 us (1%)
    all_to_all x2, blocking collectives, gather_rows(): lax.all_to_all(jnp.broadcast_to(far[None], (NNEAR,) + far.shape), NEAR, 0...  30.4 us
    all_to_all x2, blocking collectives, shards(): pieces = lax.all_to_all(pieces, GRP, 0, 0)  27.6 us
    all_to_all x2, blocking collectives, gather_rows(): far = lax.all_to_all(send, FAR, 0, 0)  27.1 us
    all_to_all x1, blocking collectives, shards(): near = lax.all_to_all(grads, NEAR, 0, 0)  18.9 us
    all_to_all x1, blocking collectives, shards(): far = lax.all_to_all(near, FAR, 0, 0)  12.5 us
    ppermute x1, starting transfers between devices, shards(): other = lax.ppermute(mine, 'c', SWAP)  9.07 us
    ppermute x1, starting transfers between devices, shards(): inputs_other = lax.ppermute(inputs, 'c', SWAP)  8.75 us
    ppermute x1, starting transfers between devices, shards(): there = lax.ppermute(sent, 'c', SWAP)  6.29 us
  transfers between devices with their start and end apart: 3, of which 2 were waited for; matrix products, arithmetic and copies ran while one was open for 1% of the time, Pallas kernels for 1%

profile of v6, /device:TPU:1, one launch (start us, length us, event | category | flops | bytes accessed | tf_op | source)
XLA Modules:
  0.0 151.7 jit_solution(5738973703217901064)
XLA Ops:
  0.6 8.7 %collective-permute-start = (bf16[256,4608]{1,0:T(8,128)(2,1)}, bf16[256,4608]{1,0:T(8,128)(2,1)S(1)}, u32[]{:S(2)}, u32[]{:S(2)}) collective-permute-start(bf16[256,4608]{1,0:T(8,128)(2,1)} %bitcast.13), channel_id=1, source_target_pairs={{0,1},{1,0},{2,3},{3,2},{4,5},{5,4},{6,7},{7,6},{8,9},{9,8},{10,11... | collective-permute-start | bytes 7077896 | tf_op jit(solution)/shard_map/ppermute | solution.py:185
  9.4 0.0 copy-start.1
  9.4 0.9 copy-done.1
  10.3 13.2 %all_to_all.40 = bf16[4,144,256]{2,1,0:T(8,128)(2,1)S(1)} all-to-all(bf16[4,144,256]{2,1,0:T(8,128)(2,1)S(1)} %cast.1), channel_id=1, replica_groups=mesh['xl'=2,'z'=8,'yh'=4,'yl'=2,'xh'=2,'c'=2] {'yh'}, dimensions={0} | all-to-all | bytes 589824 | tf_op jit(solution)/shard_map/all_to_all | solution.py:172
  23.5 0.1 broadcast_in_dim.10
  23.6 0.0 copy-start
  23.6 16.2 %all_to_all.41.weight_ref = bf16[4,4,144,256]{3,2,1,0:T(8,128)(2,1)S(1)} all-to-all(bf16[4,4,144,256]{3,2,1,0:T(8,128)(2,1)S(1)} %broadcast_in_dim.10), channel_id=1, replica_groups=mesh['xl'=2,'z'=8,'yh'=4,'yl'=2,'xh'=2,'c'=2] {'yl','xh'}, dimensions={0} | all-to-all | bytes 2359296 | tf_op jit(solution)/shard_map/all_to_all | solution.py:173
  39.8 0.0 collective-permute-done.other_ref
  39.8 1.4 pred_.1
  41.2 6.3 %collective-permute-start.1 = (bf16[2,256,256]{2,1,0:T(8,128)(2,1)S(1)}, bf16[2,256,256]{2,1,0:T(8,128)(2,1)S(1)}, u32[]{:S(2)}, u32[]{:S(2)}) collective-permute-start(bf16[2,256,256]{2,1,0:T(8,128)(2,1)S(1)} %get-tuple-element.16), channel_id=1, source_target_pairs={{0,1},{1,0},{2,3},{3,2},{4,5},{5,4},{6,7},{7,6},{8,9},{9,8},{10,11... | collective-permute-start | bytes 786440 | tf_op jit(solution)/shard_map/ppermute | solution.py:192
  47.5 0.7 turn.1.mine_ref
  48.2 0.5 collective-permute-done.1.there_ref
  48.7 1.9 %grad.1 = bf16[4,4,144,256]{3,2,1,0:T(8,128)(2,1)S(1)} custom-call(bf16[4608,256]{1,0:T(8,128)(2,1)S(1)} %turn.1.mine_ref, bf16[256,4608]{1,0:T(8,128)(2,1)S(1)} %collective-permute-done.other_ref, f32[2,256,256]{2,1,0:T(8,128)S(1)} %get-tuple-element.15.here_ref, bf16[2,256,256]{2,1,0:T(8,128)(2,1)S(1)} %collective-permute-done.1.there_ref), custom_call_target="tpu_custom_call" | custom-call | tf_op jit(solution)/shard_map/grad/pallas_call | solution.py:166
  50.6 18.9 %all_to_all.42.parts_ref = bf16[4,4,144,256]{3,2,1,0:T(8,128)(2,1)S(1)} all-to-all(bf16[4,4,144,256]{3,2,1,0:T(8,128)(2,1)S(1)} %grad.1), channel_id=1, replica_groups=mesh['xl'=2,'z'=8,'yh'=4,'yl'=2,'xh'=2,'c'=2] {'yl','xh'}, dimensions={0} | all-to-all | bytes 2359296 | tf_op jit(solution)/shard_map/all_to_all | solution.py:203
  69.5 0.1 near_sum.1
  69.6 0.0 copy-start.4
  69.7 12.5 %all_to_all.43.parts_ref = bf16[4,144,256]{2,1,0:T(8,128)(2,1)S(1)} all-to-all(bf16[4,144,256]{2,1,0:T(8,128)(2,1)S(1)} %near_sum.1), channel_id=1, replica_groups=mesh['xl'=2,'z'=8,'yh'=4,'yl'=2,'xh'=2,'c'=2] {'yh'}, dimensions={0} | all-to-all | bytes 589824 | tf_op jit(solution)/shard_map/all_to_all | solution.py:205
  82.1 0.2 delta.1
  82.3 17.4 %all_to_all.44.pieces_ref = bf16[16,16,256]{2,1,0:T(8,128)(2,1)S(1)} all-to-all(bf16[16,16,256]{2,1,0:T(8,128)(2,1)S(1)} %get-tuple-element.17), channel_id=1, replica_groups=mesh['xl'=2,'z'=8,'yh'=4,'yl'=2,'xh'=2,'c'=2] {'xl','z'}, dimensions={0} | all-to-all | bytes 262144 | tf_op jit(solution)/shard_map/all_to_all | solution.py:210
  99.7 0.6 mates.1
  100.3 10.2 %all_to_all.45.pieces_ref = bf16[16,16,256]{2,1,0:T(8,128)(2,1)S(1)} all-to-all(bf16[16,16,256]{2,1,0:T(8,128)(2,1)S(1)} %mates.1), channel_id=1, replica_groups=mesh['xl'=2,'z'=8,'yh'=4,'yl'=2,'xh'=2,'c'=2] {'xl','z'}, dimensions={0} | all-to-all | bytes 262144 | tf_op jit(solution)/shard_map/all_to_all | solution.py:212
  110.5 0.1 update.1
  110.5 13.9 %all_to_all.46 = bf16[4,144,256]{2,1,0:T(8,128)(2,1)S(1)} all-to-all(bf16[4,144,256]{2,1,0:T(8,128)(2,1)S(1)} %get-tuple-element.21), channel_id=1, replica_groups=mesh['xl'=2,'z'=8,'yh'=4,'yl'=2,'xh'=2,'c'=2] {'yh'}, dimensions={0} | all-to-all | bytes 589824 | tf_op jit(solution)/shard_map/all_to_all | solution.py:172
  124.4 0.1 broadcast_in_dim.24
  124.5 14.3 %all_to_all.47.mine_ref = bf16[4,4,144,256]{3,2,1,0:T(8,128)(2,1)S(1)} all-to-all(bf16[4,4,144,256]{3,2,1,0:T(8,128)(2,1)S(1)} %broadcast_in_dim.24), channel_id=1, replica_groups=mesh['xl'=2,'z'=8,'yh'=4,'yl'=2,'xh'=2,'c'=2] {'yl','xh'}, dimensions={0} | all-to-all | bytes 2359296 | tf_op jit(solution)/shard_map/all_to_all | solution.py:173
  138.8 9.1 %collective-permute-start.2 = (bf16[4,4,144,256]{3,2,1,0:T(8,128)(2,1)S(1)}, bf16[4,4,144,256]{3,2,1,0:T(8,128)(2,1)S(1)}, u32[]{:S(2)}, u32[]{:S(2)}) collective-permute-start(bf16[4,4,144,256]{3,2,1,0:T(8,128)(2,1)S(1)} %all_to_all.47.mine_ref), channel_id=1, source_target_pairs={{0,1},{1,0},{2,3},{3,2},{4,5},{5,4},{6,7},{7,6},{8,9},{9,8},{10,11... | collective-permute-start | bytes 3538952 | tf_op jit(solution)/shard_map/ppermute | solution.py:220
  147.8 0.7 copy.13
  148.5 0.7 copy.14
  149.2 0.1 place.1.full_ref
  149.3 1.0 collective-permute-done.2.other_ref
  150.3 0.1 copy-done.3
  150.4 1.3 rollout.1
  (14 shorter events, 0.0 us)
Async XLA Ops:
  0.6 39.2 %collective-permute-start = (bf16[256,4608]{1,0:T(8,128)(2,1)}, bf16[256,4608]{1,0:T(8,128)(2,1)S(1)}, u32[]{:S(2)}, u32[]{:S(2)}) collective-permute-start(bf16[256,4608]{1,0:T(8,128)(2,1)} %bitcast.13), channel_id=1, source_target_pairs={{0,1},{1,0},{2,3},{3,2},{4,5},{5,4},{6,7},{7,6},{8,9},{9,8},{10,11... | collective-permute-start | bytes 7077896 | tf_op jit(solution)/shard_map/ppermute | solution.py:185
  9.4 0.9 copy-start.1
  23.5 16.3 %copy-start.7 = (bf16[1,256,256]{2,1,0:T(8,128)(2,1)S(1)}, bf16[1,256,256]{2,1,0:T(8,128)(2,1)}, u32[]{:S(2)}) copy-start(bf16[1,256,256]{2,1,0:T(8,128)(2,1)} %param.13) | copy-start | bytes 393220
  23.6 16.2 %copy-start = (bf16[1,256,4608]{2,1,0:T(8,128)(2,1)S(1)}, bf16[1,256,4608]{2,1,0:T(8,128)(2,1)}, u32[]{:S(2)}) copy-start(bf16[1,256,4608]{2,1,0:T(8,128)(2,1)} %param.12) | copy-start | bytes 7077892
  41.2 7.4 %collective-permute-start.1 = (bf16[2,256,256]{2,1,0:T(8,128)(2,1)S(1)}, bf16[2,256,256]{2,1,0:T(8,128)(2,1)S(1)}, u32[]{:S(2)}, u32[]{:S(2)}) collective-permute-start(bf16[2,256,256]{2,1,0:T(8,128)(2,1)S(1)} %get-tuple-element.16), channel_id=1, source_target_pairs={{0,1},{1,0},{2,3},{3,2},{4,5},{5,4},{6,7},{7,6},{8,9},{9,8},{10,11... | collective-permute-start | bytes 786440 | tf_op jit(solution)/shard_map/ppermute | solution.py:192
  69.5 12.6 %copy-start.2 = (f32[1,144,256]{2,1,0:T(8,128)S(1)}, f32[1,144,256]{2,1,0:T(8,128)}, u32[]{:S(2)}) copy-start(f32[1,144,256]{2,1,0:T(8,128)} %param.8) | copy-start | bytes 442372
  69.5 12.6 %copy-start.5 = (f32[1,144,256]{2,1,0:T(8,128)S(1)}, f32[1,144,256]{2,1,0:T(8,128)}, u32[]{:S(2)}) copy-start(f32[1,144,256]{2,1,0:T(8,128)} %param.10) | copy-start | bytes 442372
  69.5 12.6 %copy-start.6 = (f32[1,144,256]{2,1,0:T(8,128)S(1)}, f32[1,144,256]{2,1,0:T(8,128)}, u32[]{:S(2)}) copy-start(f32[1,144,256]{2,1,0:T(8,128)} %param.11) | copy-start | bytes 442372
  69.5 30.2 %copy-start.8 = (s32[16,1]{0,1:T(1,128)S(1)}, s32[16,1]{0,1:T(1,128)}, u32[]{:S(2)}) copy-start(s32[16,1]{0,1:T(1,128)} %param.15) | copy-start | bytes 196
  69.6 40.8 %copy-start.4 = (f32[1,144,256]{2,1,0:T(8,128)S(1)}, f32[1,144,256]{2,1,0:T(8,128)}, u32[]{:S(2)}) copy-start(f32[1,144,256]{2,1,0:T(8,128)} %param.9) | copy-start | bytes 442372
  138.8 11.5 %collective-permute-start.2 = (bf16[4,4,144,256]{3,2,1,0:T(8,128)(2,1)S(1)}, bf16[4,4,144,256]{3,2,1,0:T(8,128)(2,1)S(1)}, u32[]{:S(2)}, u32[]{:S(2)}) collective-permute-start(bf16[4,4,144,256]{3,2,1,0:T(8,128)(2,1)S(1)} %all_to_all.47.mine_ref), channel_id=1, source_target_pairs={{0,1},{1,0},{2,3},{3,2},{4,5},{5,4},{6,7},{7,6},{8,9},{9,8},{10,11... | collective-permute-start | bytes 3538952 | tf_op jit(solution)/shard_map/ppermute | solution.py:220
  149.2 1.3 copy-start.3
